TPU v7x, 512 devices: a whole 4x8x8 slice. The times are simulated.
512 devices in a mesh: dp: 2 (over core), tensor: 4 (over x), expert: 64 (over y, z).
Axes of the slice: x: 4, y: 8, z: 8, core: 2. Of those that a mesh axis runs over, the one named last changes fastest.
Arguments:
- checkpoint: bfloat16 [16384, 2048], P(('dp', 'expert'), 'tensor'), may hold values from -6 to 6
- scales: float32 [16384], P(('dp', 'expert')), may hold values from 0.5 to 2
- out_grad: bfloat16 [16384, 2048], P(('dp', 'expert'), 'tensor'), may hold values from -1.5 to 1.5
- expert_ids: int32 [16384, 8], P(('dp', 'expert')), may hold values from 0 to 127, all different within a row; in each aligned block of 128 rows (0 to 127, 128 to 255, ...) at most 8 rows name the same one
- gates: float32 [16384, 8], P(('dp', 'expert')), may hold values from 0.05 to 1
- w_gate: bfloat16 [128, 768, 2048], P(('dp', 'expert'), 'tensor'), may hold values from -0.125 to 0.125
- w_up: bfloat16 [128, 768, 2048], P(('dp', 'expert'), 'tensor'), may hold values from -0.125 to 0.125
- w_down: bfloat16 [128, 768, 2048], P(('dp', 'expert'), 'tensor'), may hold values from -0.21875 to 0.21875
Outputs:
- grad_input: bfloat16 [16384, 2048], P(('dp', 'expert'), 'tensor')
- grad_gates: float32 [16384, 8], P(('dp', 'expert'))
Inputs may be any that keep to these rules, and one draw needn't show every extreme that they name: `expert_ids`: each row names 8 different experts. Among the 128 rows of one device (aligned blocks of rows), no expert is named more than 8 times, a bound that some block reaches.
All inputs are finite; a program needn't handle non-finite values.
Results may differ from a plain program's by a relative error of at most 0.012.
Values may be sent and summed in bfloat16 or wider, within the bound.
A program may use at most 64 MiB of HBM per device.

v0:
```python
import jax
import jax.numpy as jnp
from jax import lax
from jax.sharding import PartitionSpec as P


def slot_table(expert_ids, expert_count, slot_cap):
    token_rows = expert_ids.shape[0]
    pick_count = expert_ids.shape[1]
    chosen = expert_ids.reshape(-1)
    onehot = (chosen[:, None] == jnp.arange(expert_count, dtype=jnp.int32)[None, :]).astype(
        jnp.int32
    )
    earlier = jnp.cumsum(onehot, axis=0) - onehot
    position = jnp.sum(earlier * onehot, axis=1)
    slot_of = chosen * slot_cap + position
    token_ids = jnp.arange(token_rows * pick_count, dtype=jnp.int32) // pick_count
    owner = jnp.full((expert_count * slot_cap,), token_rows, jnp.int32).at[slot_of].set(token_ids)
    return (slot_of, owner)


def finish(gate_pre, up_pre, back, weight_gate, weight_up):
    sigma = jax.nn.sigmoid(gate_pre)
    swish = gate_pre * sigma
    hidden = (swish * up_pre).astype(jnp.bfloat16)
    gate_part = jnp.sum(hidden.astype(jnp.float32) * back, axis=1).astype(jnp.bfloat16)
    d_gate = (back * up_pre * sigma * (1.0 + gate_pre * (1.0 - sigma))).astype(jnp.bfloat16)
    d_up = (back * swish).astype(jnp.bfloat16)
    input_part = jnp.dot(d_gate, weight_gate, preferred_element_type=jnp.float32)
    input_part = input_part + jnp.dot(d_up, weight_up, preferred_element_type=jnp.float32)
    return (input_part.astype(jnp.bfloat16), gate_part)


def close_expert(input_part, gate_part, sources, items, model_width):
    shaped = input_part.reshape(sources, items, model_width)
    gate_shaped = gate_part.reshape(sources, items)
    return (shaped, gate_shaped)


def body(checkpoint, scales, out_grad, expert_ids, gates, w_gate, w_up, w_down):
    expert_count = lax.axis_size("dp") * lax.axis_size("expert")
    token_rows = checkpoint.shape[0]
    pick_count = expert_ids.shape[1]
    slot_cap = min(token_rows, token_rows * pick_count // expert_count)
    weight_gate = w_gate[0]
    weight_up = w_up[0]
    weight_down = w_down[0]
    model_width = weight_gate.shape[1]
    contract = (((1,), (1,)), ((), ()))
    dequant = (checkpoint.astype(jnp.float32) * scales[:, None]).astype(jnp.bfloat16)
    slot_of, owner = slot_table(expert_ids, expert_count, slot_cap)
    full_x, full_grad = (
        lax.all_gather(dequant, "tensor", axis=1, tiled=True),
        lax.all_gather(out_grad, "tensor", axis=1, tiled=True),
    )
    send_x = jnp.take(full_x, owner, axis=0, mode="fill", fill_value=0).reshape(
        expert_count, slot_cap, model_width
    )
    send_grad = jnp.take(full_grad, owner, axis=0, mode="fill", fill_value=0).reshape(
        expert_count, slot_cap, model_width
    )
    rows_in = lax.all_to_all(send_x, ("dp", "expert"), split_axis=0, concat_axis=0, tiled=True)
    grads_in = lax.all_to_all(send_grad, ("dp", "expert"), split_axis=0, concat_axis=0, tiled=True)
    sources, items, width = rows_in.shape
    rows_flat = rows_in.reshape(sources * items, width)
    grads_flat = grads_in.reshape(sources * items, width)
    gate_pre = lax.dot_general(rows_flat, weight_gate, contract, preferred_element_type=jnp.float32)
    up_pre = lax.dot_general(rows_flat, weight_up, contract, preferred_element_type=jnp.float32)
    back = lax.dot_general(grads_flat, weight_down, contract, preferred_element_type=jnp.float32)
    input_part, gate_part = finish(gate_pre, up_pre, back, weight_gate, weight_up)
    input_part, gate_part = close_expert(input_part, gate_part, sources, items, model_width)
    back_input, back_gate = (
        lax.all_to_all(input_part, ("dp", "expert"), split_axis=0, concat_axis=0, tiled=True),
        lax.all_to_all(gate_part, ("dp", "expert"), split_axis=0, concat_axis=0, tiled=True),
    )
    picked = jnp.take(back_input.reshape(expert_count * slot_cap, model_width), slot_of, axis=0)
    picked = picked.astype(jnp.float32).reshape(token_rows, pick_count, model_width)
    pair_sums = lax.psum_scatter(
        picked.astype(jnp.bfloat16), "tensor", scatter_dimension=2, tiled=True
    )
    rounded = lax.optimization_barrier(pair_sums).astype(jnp.float32)
    weighted = jnp.sum(rounded * gates[:, :, None], axis=1)
    gate_pairs = (
        jnp.take(back_gate.reshape(-1), slot_of, axis=0)
        .astype(jnp.float32)
        .reshape(token_rows, pick_count)
    )
    gate_out = lax.psum(gate_pairs.astype(jnp.bfloat16), "tensor").astype(jnp.float32)
    return (weighted.astype(jnp.bfloat16), gate_out)


def solution(mesh):
    return jax.shard_map(
        body,
        mesh=mesh,
        in_specs=(
            P(("dp", "expert"), "tensor"),
            P(("dp", "expert")),
            P(("dp", "expert"), "tensor"),
            P(("dp", "expert"), None),
            P(("dp", "expert"), None),
            P(("dp", "expert"), "tensor", None),
            P(("dp", "expert"), "tensor", None),
            P(("dp", "expert"), "tensor", None),
        ),
        out_specs=(P(("dp", "expert"), "tensor"), P(("dp", "expert"), None)),
        check_vma=False,
    )
```

profile of v0, /device:TPU:1, one launch (start us, length us, event | category | flops | bytes accessed | tf_op | source)
XLA Modules:
  0.0 566.6 jit_solution(6533605995353139304)
XLA Ops:
  9.3 4.3 scatter_custom_fusion
  14.6 11.1 %all_gather.7 = bf16[128,2048]{1,0:T(8,128)(2,1)S(1)} all-gather(bf16[128,512]{1,0:T(8,128)(2,1)S(1)} %multiply_convert_fusion.5), channel_id=1, replica_groups=mesh['dp'=2,'tensor'=4,'expert'=64] {'tensor'}, dimensions={1}, use_global_device_ids=true | all-gather | bytes 655360 | tf_op jit(solution)/shard_map/all_gather | solution.py:53
  25.7 9.9 %all_gather.6 = bf16[128,2048]{1,0:T(8,128)(2,1)S(1)} all-gather(bf16[128,512]{1,0:T(8,128)(2,1)S(1)} %copy-done.3), channel_id=1, replica_groups=mesh['dp'=2,'tensor'=4,'expert'=64] {'tensor'}, dimensions={1}, use_global_device_ids=true | all-gather | bytes 655360 | tf_op jit(solution)/shard_map/all_gather | solution.py:54
  35.6 6.1 %gather_fusion.3 = bf16[1024,2048]{1,0:T(8,128)(2,1)} fusion(bf16[128,2048]{1,0:T(8,128)(2,1)S(1)} %all_gather.7, s32[1024]{0:T(1024)S(1)} %fusion.24), kind=kCustom, calls=%fused_computation.1.clone | custom fusion | bytes 8392704 | tf_op jit(solution)/shard_map/jit(_take)/gather | solution.py:56
  41.6 6.0 %gather_fusion.2 = bf16[1024,2048]{1,0:T(8,128)(2,1)} fusion(bf16[128,2048]{1,0:T(8,128)(2,1)S(1)} %all_gather.6, s32[1024]{0:T(1024)S(1)} %fusion.24), kind=kCustom, calls=%fused_computation.clone | custom fusion | bytes 8392704 | tf_op jit(solution)/shard_map/jit(_take)/gather | solution.py:59
  47.6 5.3 select_bitcast_fusion.1
  52.9 134.2 %all_to_all.21 = bf16[128,8,2048]{2,1,0:T(8,128)(2,1)} all-to-all(bf16[128,8,2048]{2,1,0:T(8,128)(2,1)S(1)} %get-tuple-element.10), channel_id=1, replica_groups=mesh['dp'=2,'tensor'=4,'expert'=64] {'dp','expert'}, dimensions={0} | all-to-all | bytes 8388608 | tf_op jit(solution)/shard_map/all_to_all | solution.py:62
  187.2 23.7 %all-to-all-start = ((bf16[128,8,2048]{2,1,0:T(8,128)(2,1)}), bf16[128,8,2048]{2,1,0:T(8,128)(2,1)}, u32[]{:S(2)}, u32[]{:S(2)}) async-start(bf16[128,8,2048]{2,1,0:T(8,128)(2,1)} %get-tuple-element.9), calls=%async_computation | async-start | bytes 8388608 | tf_op jit(solution)/shard_map/all_to_all | solution.py:63
  210.9 3.9 fusion
  214.8 1.6 fusion.2
  216.4 106.1 %all-to-all-done = bf16[128,8,2048]{2,1,0:T(8,128)(2,1)} async-done(((bf16[128,8,2048]{2,1,0:T(8,128)(2,1)}), bf16[128,8,2048]{2,1,0:T(8,128)(2,1)}, u32[]{:S(2)}, u32[]{:S(2)}) %all-to-all-start) | async-done | bytes 4194336 | tf_op jit(solution)/shard_map/all_to_all | solution.py:63
  322.5 4.0 multiply_reduce_fusion.1
  326.5 4.7 fusion.7
  331.9 12.9 %all-to-all-start.3 = ((bf16[128,1,8]{2,1,0:T(2,128)(2,1)}), bf16[128,1,8]{2,1,0:T(2,128)(2,1)S(1)}, u32[]{:S(2)}, u32[]{:S(2)}) async-start(bf16[128,1,8]{2,1,0:T(2,128)(2,1)} %convert_element_type.71), calls=%async_computation.4 | async-start | bytes 131072 | tf_op jit(solution)/shard_map/all_to_all | solution.py:74
  344.8 6.9 %fusion.6 = bf16[128,8,2048]{2,1,0:T(8,128)(2,1)} fusion(f32[1024,2048]{1,0:T(8,128)} %fusion.7, bf16[1,192,2048]{2,1,0:T(8,128)(2,1)} %param.16, f32[1024,192]{0,1:T(8,128)S(1)} %get-tuple-element.12, f32[1024,192]{0,1:T(8,128)S(1)} %fusion), kind=kOutput, calls=%fused_computation.15 | convolution fusion | flops 810680320 | bytes 14942208 | tf_op jit(solution)/shard_map/dot_general | solution.py:30
  351.8 4.9 all-to-all-done.3
  356.7 9.2 %all-to-all-start.2 = ((bf16[128,8,2048]{2,1,0:T(8,128)(2,1)}), bf16[128,8,2048]{2,1,0:T(8,128)(2,1)}, u32[]{:S(2)}, u32[]{:S(2)}) async-start(bf16[128,8,2048]{2,1,0:T(8,128)(2,1)} %fusion.6), calls=%async_computation.2 | async-start | bytes 8388608 | tf_op jit(solution)/shard_map/all_to_all | solution.py:73
  366.5 6.8 %gather_fusion.1 = bf16[1024]{0:T(1024)(128)(2,1)S(1)} fusion(bf16[1024]{0:T(1024)(128)(2,1)S(1)} %reshape.121, s32[1024]{0:T(1024)S(1)} %broadcast_clamp_fusion), kind=kCustom, calls=%fused_computation.3 | custom fusion | bytes 8192 | tf_op jit(solution)/shard_map/jit(_take)/gather | solution.py:84
  373.5 102.2 %all-to-all-done.2 = bf16[128,8,2048]{2,1,0:T(8,128)(2,1)} async-done(((bf16[128,8,2048]{2,1,0:T(8,128)(2,1)}), bf16[128,8,2048]{2,1,0:T(8,128)(2,1)}, u32[]{:S(2)}, u32[]{:S(2)}) %all-to-all-start.2) | async-done | bytes 4194336 | tf_op jit(solution)/shard_map/all_to_all | solution.py:73
  475.7 11.6 %gather_fusion = bf16[1024,2048]{1,0:T(8,128)(2,1)} fusion(bf16[1024,2048]{1,0:T(8,128)(2,1)} %bitcast.13, s32[1024]{0:T(1024)S(1)} %broadcast_clamp_fusion), kind=kCustom, calls=%fused_computation.2 | custom fusion | bytes 8392704 | tf_op jit(solution)/shard_map/jit(_take)/gather | solution.py:76
  487.2 4.6 bitcast_select_fusion
  492.6 13.9 %psum.7 = bf16[128,8]{1,0:T(8,128)(2,1)S(1)} all-reduce(bf16[128,8]{1,0:T(8,128)(2,1)S(1)} %get-tuple-element.7), channel_id=1, replica_groups=mesh['dp'=2,'tensor'=4,'expert'=64] {'tensor'}, use_global_device_ids=true, to_apply=%region_7.9 | all-reduce | flops 1024 | bytes 4096 | tf_op jit(solution)/shard_map/psum | solution.py:88
  507.2 50.0 %reduce-scatter.2.cloned.1.call-done = bf16[128,8,512]{2,1,0:T(8,128)(2,1)} async-done(((bf16[128,8,2048]{2,1,0:T(8,128)(2,1)}), bf16[128,8,512]{2,1,0:T(8,128)(2,1)}) %reduce-scatter.2.cloned.1.call-update) | async-done | bytes 1048592 | tf_op jit(solution)/shard_map/reduce_scatter | solution.py:78
  557.2 2.6 multiply_reduce_fusion
  (39 shorter events, 6.0 us)
Async XLA Ops:
  7.2 203.7 %copy-start = (bf16[1,192,2048]{2,1,0:T(8,128)(2,1)S(1)}, bf16[1,192,2048]{2,1,0:T(8,128)(2,1)}, u32[]{:S(2)}) copy-start(bf16[1,192,2048]{2,1,0:T(8,128)(2,1)} %param.15) | copy-start | bytes 2359300
  7.2 18.5 %copy-start.3 = (bf16[128,512]{1,0:T(8,128)(2,1)S(1)}, bf16[128,512]{1,0:T(8,128)(2,1)}, u32[]{:S(2)}) copy-start(bf16[128,512]{1,0:T(8,128)(2,1)} %param.12) | copy-start | bytes 393220
  187.2 135.3 %all-to-all-start = ((bf16[128,8,2048]{2,1,0:T(8,128)(2,1)}), bf16[128,8,2048]{2,1,0:T(8,128)(2,1)}, u32[]{:S(2)}, u32[]{:S(2)}) async-start(bf16[128,8,2048]{2,1,0:T(8,128)(2,1)} %get-tuple-element.9), calls=%async_computation | async-start | bytes 8388608 | tf_op jit(solution)/shard_map/all_to_all | solution.py:63
  210.9 3.9 copy-start.1
  210.9 3.9 copy-start.2
  331.9 24.8 %all-to-all-start.3 = ((bf16[128,1,8]{2,1,0:T(2,128)(2,1)}), bf16[128,1,8]{2,1,0:T(2,128)(2,1)S(1)}, u32[]{:S(2)}, u32[]{:S(2)}) async-start(bf16[128,1,8]{2,1,0:T(2,128)(2,1)} %convert_element_type.71), calls=%async_computation.4 | async-start | bytes 131072 | tf_op jit(solution)/shard_map/all_to_all | solution.py:74
  356.7 119.0 %all-to-all-start.2 = ((bf16[128,8,2048]{2,1,0:T(8,128)(2,1)}), bf16[128,8,2048]{2,1,0:T(8,128)(2,1)}, u32[]{:S(2)}, u32[]{:S(2)}) async-start(bf16[128,8,2048]{2,1,0:T(8,128)(2,1)} %fusion.6), calls=%async_computation.2 | async-start | bytes 8388608 | tf_op jit(solution)/shard_map/all_to_all | solution.py:73
  365.9 191.3 %reduce-scatter.2.cloned.1.call-start = ((), (), s32[]{:S(2)}) async-start(), calls=%async_computation.5 | async-start | bytes 5242880 | tf_op jit(solution)/shard_map/reduce_scatter | solution.py:78
  491.8 0.7 copy-start.4
Sparse Core Ops, SparseCore 0:
  491.9 65.1 reduce-scatter.1
where the time goes:
time: 567 us
  waiting for transfers between devices  263 us (46%)
  blocking collectives  169 us (30%)
  starting transfers between devices  46 us (8%)
  local copies, waits for them, and re-layouts  38.6 us (7%)
  matrix products  21 us (4%)
  other arithmetic  14.3 us (3%)
  between operations  14.3 us (3%)
    all_to_all x1, blocking collectives, body(): lax.all_to_all(send_x, ('dp', 'expert'), split_axis=0, concat_axis=0, til...  134 us
    all_to_all x1, waiting for transfers between devices, body(): lax.all_to_all(send_grad, ('dp', 'expert'), split_axis=0, concat_axis=0,...  106 us
    all_to_all x1, waiting for transfers between devices, body(): lax.all_to_all(input_part, ('dp', 'expert'), split_axis=0, concat_axis=0,...  102 us
    reduce_scatter x1, waiting for transfers between devices, body(): lax.psum_scatter(picked.astype(jnp.bfloat16), 'tensor', scatter_dimension...  50 us
    all_to_all x1, starting transfers between devices, body(): lax.all_to_all(send_grad, ('dp', 'expert'), split_axis=0, concat_axis=0,...  23.7 us
    psum x1, blocking collectives, body(): lax.psum(gate_pairs.astype(jnp.bfloat16), 'tensor').astype(jnp.float32)  13.9 us
    all_to_all x1, starting transfers between devices, body(): lax.all_to_all(gate_part, ('dp', 'expert'), split_axis=0, concat_axis=0,...  12.9 us
    gather x1, local copies, waits for them, and re-layouts, body(): jnp.take(back_input.reshape(expert_count * slot_cap, model_width), slot_o...  11.6 us
  transfers between devices with their start and end apart: 4, of which 4 were waited for; matrix products, arithmetic and copies ran while one was open for 4% of the time, Pallas kernels for 0%

commit v1 on v0

v1 whole, which is shorter than its diff:
```python
import jax
import jax.numpy as jnp
from jax import lax
from jax.sharding import PartitionSpec as P


def body(checkpoint, scales, out_grad, expert_ids, gates, w_gate, w_up, w_down):
    f32, bf16 = jnp.float32, jnp.bfloat16
    planes = lax.axis_size("tensor")
    experts = lax.axis_size("dp") * lax.axis_size("expert")
    rank = lax.axis_index("tensor")
    tokens, part = checkpoint.shape
    picks = expert_ids.shape[1]
    cap = tokens * picks // experts
    own = cap // planes
    width = part * planes
    wg = lax.all_gather(w_gate[0], "tensor", axis=0, tiled=True)
    wu = lax.all_gather(w_up[0], "tensor", axis=0, tiled=True)
    wd = lax.all_gather(w_down[0], "tensor", axis=0, tiled=True)
    dequant = (checkpoint.astype(f32) * scales[:, None]).astype(bf16)
    both = lax.all_gather(jnp.stack([dequant, out_grad]), "tensor", axis=2, tiled=True)

    named = expert_ids[:, :, None] == jnp.arange(experts, dtype=jnp.int32)[None, None, :]
    member = jnp.any(named, axis=1)
    weight = jnp.sum(jnp.where(named, gates[:, :, None], 0.0), axis=1)
    lower = (jnp.arange(tokens)[:, None] > jnp.arange(tokens)[None, :]).astype(bf16)
    place = jnp.dot(lower, member.astype(bf16), preferred_element_type=f32).astype(jnp.int32)
    slots = rank * own + jnp.arange(own, dtype=jnp.int32)
    pick = (member.T[:, None, :] & (place.T[:, None, :] == slots[None, :, None]))
    pick_rows = pick.reshape(experts * own, tokens)
    one = pick_rows.astype(bf16)
    send_x = jnp.dot(one, both[0], preferred_element_type=f32).astype(bf16)
    send_g = jnp.dot(one, both[1], preferred_element_type=f32).astype(bf16)
    names = ("dp", "expert")
    rows = lax.all_to_all(send_x.reshape(experts, own, width), names, 0, 0, tiled=True)
    grads = lax.all_to_all(send_g.reshape(experts, own, width), names, 0, 0, tiled=True)
    rows = rows.reshape(experts * own, width)
    grads = grads.reshape(experts * own, width)
    contract = (((1,), (1,)), ((), ()))
    gate_pre = lax.dot_general(rows, wg, contract, preferred_element_type=f32)
    up_pre = lax.dot_general(rows, wu, contract, preferred_element_type=f32)
    back = lax.dot_general(grads, wd, contract, preferred_element_type=f32)
    sigma = jax.nn.sigmoid(gate_pre)
    swish = gate_pre * sigma
    hidden = (swish * up_pre).astype(bf16)
    gate_term = jnp.sum(hidden.astype(f32) * back, axis=1)
    d_gate = (back * up_pre * sigma * (1.0 + gate_pre * (1.0 - sigma))).astype(bf16)
    d_up = (back * swish).astype(bf16)
    result = jnp.dot(d_gate, wg, preferred_element_type=f32)
    result = result + jnp.dot(d_up, wu, preferred_element_type=f32)
    tail = jnp.broadcast_to(gate_term[:, None], (experts * own, 128))
    packed = jnp.concatenate([result.astype(bf16), tail.astype(bf16)], axis=1)
    came = lax.all_to_all(packed.reshape(experts, own, width + 128), names, 0, 0, tiled=True)
    came = came.reshape(experts * own, width + 128)
    combine = jnp.where(pick, weight.T[:, None, :], 0.0).reshape(experts * own, tokens)
    high = combine.astype(bf16)
    low = (combine - high.astype(f32)).astype(bf16)
    flip = (((0,), (0,)), ((), ()))
    mixed = lax.dot_general(high, came[:, :width], flip, preferred_element_type=f32)
    mixed = mixed + lax.dot_general(low, came[:, :width], flip, preferred_element_type=f32)
    term = jnp.sum(jnp.where(pick, came[:, width].astype(f32).reshape(experts, own)[:, :, None], 0.0), axis=1)
    terms = jnp.sum(jnp.where(named, term.T[:, None, :], 0.0), axis=2)
    terms = jnp.pad(terms, ((0, 0), (0, 128 - picks))).astype(bf16)
    joined = jnp.concatenate(
        [mixed.astype(bf16).reshape(tokens, planes, part), jnp.broadcast_to(terms[:, None], (tokens, planes, 128))],
        axis=2,
    ).transpose(1, 0, 2)
    summed = lax.psum_scatter(joined, "tensor", scatter_dimension=0, tiled=True)[0]
    return summed[:, :part], summed[:, part : part + picks].astype(f32)


def solution(mesh):
    return jax.shard_map(
        body,
        mesh=mesh,
        in_specs=(
            P(("dp", "expert"), "tensor"),
            P(("dp", "expert")),
            P(("dp", "expert"), "tensor"),
            P(("dp", "expert"), None),
            P(("dp", "expert"), None),
            P(("dp", "expert"), "tensor", None),
            P(("dp", "expert"), "tensor", None),
            P(("dp", "expert"), "tensor", None),
        ),
        out_specs=(P(("dp", "expert"), "tensor"), P(("dp", "expert"), None)),
        check_vma=False,
    )
```

time: 567 us -> 276 us (0.49)
  blocking collectives: 169 us -> 0 us
  waiting for transfers between devices: 263 us -> 190 us
  local copies, waits for them, and re-layouts: 38.6 us -> 9.56 us
  other arithmetic: 14.3 us -> 6.24 us
  starting transfers between devices: 46 us -> 38.9 us
    all_to_all x1 -> x0, blocking collectives: 134 us -> none  [body(): lax.all_to_all(send_x, ('dp', 'expert'), split_axis=0, concat_axis=0, til...]
    all_to_all x3, waiting for transfers between devices: 213 us -> 92.2 us  [the longest x1 32.3 us: body(): lax.all_to_all(packed.reshape(experts, own, width + 128), names, 0, 0, ti...]
    all_gather x0 -> x4, waiting for transfers between devices: none -> 77.1 us  [the longest x1 43.1 us: body(): wd = lax.all_gather(w_down[0], 'tensor', axis=0, tiled=True)]
    reduce_scatter x1, waiting for transfers between devices: 50 us -> 18.6 us  [body(): lax.psum_scatter(joined, 'tensor', scatter_dimension=0, tiled=True)[0]]
    gather x5 -> x0, local copies, waits for them, and re-layouts: 30.5 us -> none  [the longest x1 11.6 us: body(): jnp.take(back_input.reshape(expert_count * slot_cap, model_width), slot_o...]
    all_gather x2 -> x0, blocking collectives: 21 us -> none  [the longest x1 11.1 us: body(): lax.all_gather(dequant, 'tensor', axis=1, tiled=True)]
    psum x1 -> x0, blocking collectives: 13.9 us -> none  [body(): lax.psum(gate_pairs.astype(jnp.bfloat16), 'tensor').astype(jnp.float32)]
    all_to_all x3, starting transfers between devices: 45.8 us -> 38.7 us  [the longest x1 16.7 us: body(): lax.all_to_all(send_x.reshape(experts, own, width), names, 0, 0, tiled=True)]
  transfers between devices with their start and end apart: 4 -> 8, of which waited for: 4 -> 7; matrix products, arithmetic and copies ran while one was open for 4% -> 5% of each run, Pallas kernels for 0% -> 0%
where the time goes in v1:
time: 276 us; the launch traced here: 274 us
  waiting for transfers between devices  190 us (69%)
  starting transfers between devices  38.9 us (14%)
  matrix products  15.4 us (6%)
  between operations  14.1 us (5%)
  local copies, waits for them, and re-layouts  9.56 us (3%)
  other arithmetic  6.24 us (2%)
    all_gather x1, waiting for transfers between devices, body(): wd = lax.all_gather(w_down[0], 'tensor', axis=0, tiled=True)  43.1 us
    all_to_all x1, waiting for transfers between devices, body(): lax.all_to_all(packed.reshape(experts, own, width + 128), names, 0, 0, ti...  32.3 us
    all_to_all x1, waiting for transfers between devices, body(): lax.all_to_all(send_g.reshape(experts, own, width), names, 0, 0, tiled=True)  31 us
    all_gather x1, waiting for transfers between devices, body(): lax.all_gather(jnp.stack([dequant, out_grad]), 'tensor', axis=2, tiled=True)  30.6 us
    all_to_all x1, waiting for transfers between devices, body(): lax.all_to_all(send_x.reshape(experts, own, width), names, 0, 0, tiled=True)  28.9 us
    reduce_scatter x1, waiting for transfers between devices, body(): lax.psum_scatter(joined, 'tensor', scatter_dimension=0, tiled=True)[0]  18.6 us
    all_to_all x1, starting transfers between devices, body(): lax.all_to_all(send_x.reshape(experts, own, width), names, 0, 0, tiled=True)  16.7 us
    all_to_all x1, starting transfers between devices, body(): lax.all_to_all(packed.reshape(experts, own, width + 128), names, 0, 0, ti...  15 us
  transfers between devices with their start and end apart: 8, of which 7 were waited for; matrix products, arithmetic and copies ran while one was open for 5% of the time, Pallas kernels for 0%

profile of v1, /device:TPU:1, one launch (start us, length us, event | category | flops | bytes accessed | tf_op | source)
XLA Modules:
  0.0 274.1 jit_solution(13853421694187391772)
XLA Ops:
  7.2 1.0 fusion.24
  8.2 1.6 pad_maximum_fusion.1
  12.3 30.6 %all-gather.8.cloned.1.call-done = bf16[2,128,2048]{2,1,0:T(8,128)(2,1)} async-done(((bf16[2,128,512]{2,1,0:T(8,128)(2,1)}), bf16[2,128,2048]{2,1,0:T(8,128)(2,1)}) %all-gather.8.cloned.1.call-update) | async-done | bytes 1048592 | tf_op jit(solution)/shard_map/all_gather | solution.py:21
  42.9 1.5 convolution_convert_fusion
  44.4 1.5 reshape.113
  45.9 16.7 %all-to-all-start.1 = ((bf16[128,2,2048]{2,1,0:T(2,128)(2,1)}), bf16[128,2,2048]{2,1,0:T(2,128)(2,1)S(1)}, u32[]{:S(2)}, u32[]{:S(2)}) async-start(bf16[128,2,2048]{2,1,0:T(2,128)(2,1)} %reshape.113), calls=%async_computation.1 | async-start | bytes 2097152 | tf_op jit(solution)/shard_map/all_to_all | solution.py:35
  63.6 1.5 reshape.111
  65.1 28.9 %all-to-all-done.1 = bf16[128,2,2048]{2,1,0:T(2,128)(2,1)S(1)} async-done(((bf16[128,2,2048]{2,1,0:T(2,128)(2,1)}), bf16[128,2,2048]{2,1,0:T(2,128)(2,1)S(1)}, u32[]{:S(2)}, u32[]{:S(2)}) %all-to-all-start.1) | async-done | bytes 1048608 | tf_op jit(solution)/shard_map/all_to_all | solution.py:35
  94.0 7.1 %all-to-all-start = ((bf16[128,2,2048]{2,1,0:T(2,128)(2,1)}), bf16[128,2,2048]{2,1,0:T(2,128)(2,1)S(1)}, u32[]{:S(2)}, u32[]{:S(2)}) async-start(bf16[128,2,2048]{2,1,0:T(2,128)(2,1)} %reshape.111), calls=%async_computation | async-start | bytes 2097152 | tf_op jit(solution)/shard_map/all_to_all | solution.py:36
  101.6 31.0 %all-to-all-done = bf16[128,2,2048]{2,1,0:T(2,128)(2,1)S(1)} async-done(((bf16[128,2,2048]{2,1,0:T(2,128)(2,1)}), bf16[128,2,2048]{2,1,0:T(2,128)(2,1)S(1)}, u32[]{:S(2)}, u32[]{:S(2)}) %all-to-all-start) | async-done | bytes 1048608 | tf_op jit(solution)/shard_map/all_to_all | solution.py:36
  133.0 3.0 %fusion.2 = f32[256,768]{1,0:T(8,128)S(1)} fusion(bf16[256,2048]{1,0:T(8,128)(2,1)S(1)} %reshape.114, bf16[1,768,2048]{2,1,0:T(8,128)(2,1)} %all-gather.14.cloned.1.call-done), kind=kOutput, calls=%fused_computation.2 | convolution fusion | flops 805306368 | bytes 4980736 | tf_op jit(solution)/shard_map/dot_general | solution.py:40
  136.0 3.4 %all-gather.12.cloned.1.call-done = bf16[1,768,2048]{2,1,0:T(8,128)(2,1)} async-done(((bf16[1,192,2048]{2,1,0:T(8,128)(2,1)}), bf16[1,768,2048]{2,1,0:T(8,128)(2,1)}) %all-gather.12.cloned.1.call-update) | async-done | bytes 3145744 | tf_op jit(solution)/shard_map/all_gather | solution.py:18
  139.4 3.9 %fusion.6 = f32[256,768]{1,0:T(8,128)} fusion(bf16[256,2048]{1,0:T(8,128)(2,1)S(1)} %reshape.114, bf16[1,768,2048]{2,1,0:T(8,128)(2,1)} %all-gather.12.cloned.1.call-done), kind=kOutput, calls=%fused_computation.6 | convolution fusion | flops 805306368 | bytes 4980736 | tf_op jit(solution)/shard_map/dot_general | solution.py:41
  143.3 43.1 %all-gather.10.cloned.1.call-done = bf16[1,768,2048]{2,1,0:T(8,128)(2,1)} async-done(((bf16[1,192,2048]{2,1,0:T(8,128)(2,1)}), bf16[1,768,2048]{2,1,0:T(8,128)(2,1)}) %all-gather.10.cloned.1.call-update) | async-done | bytes 3145744 | tf_op jit(solution)/shard_map/all_gather | solution.py:19
  186.4 3.4 %multiply_reduce_fusion = (bf16[256]{0:T(256)(128)(2,1)S(1)}, f32[256,768]{1,0:T(8,128)S(1)}) fusion(f32[256,768]{1,0:T(8,128)} %fusion.6, f32[256,768]{1,0:T(8,128)S(1)} %fusion.2, bf16[256,2048]{1,0:T(8,128)(2,1)S(1)} %reshape.112, bf16[1,768,2048]{2,1,0:T(8,128)(2,1)} %all-gather.10.cloned.1.call-done), kind=kOutput, calls=%fused_computation.21 | convolution fusion | flops 807075584 | bytes 6554112 | tf_op jit(solution)/shard_map/dot_general | solution.py:42
  189.8 1.2 fusion
  191.7 1.1 fusion.13
  193.0 1.3 reshape.115
  194.3 15.0 %all-to-all-start.2 = ((bf16[128,2,2176]{2,1,0:T(2,128)(2,1)}), bf16[128,2,2176]{2,1,0:T(2,128)(2,1)S(1)}, u32[]{:S(2)}, u32[]{:S(2)}) async-start(bf16[128,2,2176]{2,1,0:T(2,128)(2,1)} %reshape.115), calls=%async_computation.2 | async-start | bytes 2228224 | tf_op jit(solution)/shard_map/all_to_all | solution.py:53
  209.7 32.3 %all-to-all-done.2 = bf16[128,2,2176]{2,1,0:T(2,128)(2,1)S(1)} async-done(((bf16[128,2,2176]{2,1,0:T(2,128)(2,1)}), bf16[128,2,2176]{2,1,0:T(2,128)(2,1)S(1)}, u32[]{:S(2)}, u32[]{:S(2)}) %all-to-all-start.2) | async-done | bytes 1114144 | tf_op jit(solution)/shard_map/all_to_all | solution.py:53
  245.1 0.9 maximum_bitcast_fusion
  246.0 18.6 %reduce-scatter.2.cloned.1.call-done = bf16[1,128,640]{1,2,0:T(8,128)(2,1)} async-done(((bf16[4,128,640]{1,2,0:T(8,128)(2,1)}), bf16[1,128,640]{1,2,0:T(8,128)(2,1)}) %reduce-scatter.2.cloned.1.call-update) | async-done | bytes 163856 | tf_op jit(solution)/shard_map/reduce_scatter | solution.py:68
  264.7 0.9 slice.29
  265.6 1.3 slice_convert_fusion
  (56 shorter events, 9.5 us)
Async XLA Ops:
  7.2 4.2 %copy-start.1 = (s32[128,8]{0,1:T(8,128)S(1)}, s32[128,8]{0,1:T(8,128)}, u32[]{:S(2)}) copy-start(s32[128,8]{0,1:T(8,128)} %param.11) | copy-start | bytes 12292
  7.2 35.8 %all-gather.8.cloned.1.call-start = ((), (), s32[]{:S(2)}) async-start(), calls=%async_computation.4 | async-start | bytes 1310720 | tf_op jit(solution)/shard_map/all_gather | solution.py:21
  9.9 123.1 %all-gather.14.cloned.1.call-start = ((), (), s32[]{:S(2)}) async-start(), calls=%async_computation.8 | async-start | bytes 3932160 | tf_op jit(solution)/shard_map/all_gather | solution.py:17
  10.6 128.8 %all-gather.12.cloned.1.call-start = ((), (), s32[]{:S(2)}) async-start(), calls=%async_computation.7 | async-start | bytes 3932160 | tf_op jit(solution)/shard_map/all_gather | solution.py:18
  44.4 18.8 %copy-start = (bf16[2,128,2048]{2,1,0:T(8,128)(2,1)S(1)}, bf16[2,128,2048]{2,1,0:T(8,128)(2,1)}, u32[]{:S(2)}) copy-start(bf16[2,128,2048]{2,1,0:T(8,128)(2,1)} %all-gather.8.cloned.1.call-done) | copy-start | bytes 3145732
  45.9 48.1 %all-to-all-start.1 = ((bf16[128,2,2048]{2,1,0:T(2,128)(2,1)}), bf16[128,2,2048]{2,1,0:T(2,128)(2,1)S(1)}, u32[]{:S(2)}, u32[]{:S(2)}) async-start(bf16[128,2,2048]{2,1,0:T(2,128)(2,1)} %reshape.113), calls=%async_computation.1 | async-start | bytes 2097152 | tf_op jit(solution)/shard_map/all_to_all | solution.py:35
  62.6 123.8 %all-gather.10.cloned.1.call-start = ((), (), s32[]{:S(2)}) async-start(), calls=%async_computation.6 | async-start | bytes 3932160 | tf_op jit(solution)/shard_map/all_gather | solution.py:19
  94.0 38.5 %all-to-all-start = ((bf16[128,2,2048]{2,1,0:T(2,128)(2,1)}), bf16[128,2,2048]{2,1,0:T(2,128)(2,1)S(1)}, u32[]{:S(2)}, u32[]{:S(2)}) async-start(bf16[128,2,2048]{2,1,0:T(2,128)(2,1)} %reshape.111), calls=%async_computation | async-start | bytes 2097152 | tf_op jit(solution)/shard_map/all_to_all | solution.py:36
  186.4 3.4 %copy-start.3 = (bf16[1,768,2048]{2,1,0:T(8,128)(2,1)S(1)}, bf16[1,768,2048]{2,1,0:T(8,128)(2,1)}, u32[]{:S(2)}) copy-start(bf16[1,768,2048]{2,1,0:T(8,128)(2,1)} %all-gather.14.cloned.1.call-done) | copy-start | bytes 9437188
  186.4 3.4 %copy-start.5 = (f32[256,768]{1,0:T(8,128)S(1)}, f32[256,768]{1,0:T(8,128)}, u32[]{:S(2)}) copy-start(f32[256,768]{1,0:T(8,128)} %fusion.6) | copy-start | bytes 2359300
  189.8 1.9 copy-start.4
  193.0 16.3 %copy-start.2 = (f32[128,8]{0,1:T(8,128)S(1)}, f32[128,8]{0,1:T(8,128)}, u32[]{:S(2)}) copy-start(f32[128,8]{0,1:T(8,128)} %param.12) | copy-start | bytes 12292
  194.3 47.7 %all-to-all-start.2 = ((bf16[128,2,2176]{2,1,0:T(2,128)(2,1)}), bf16[128,2,2176]{2,1,0:T(2,128)(2,1)S(1)}, u32[]{:S(2)}, u32[]{:S(2)}) async-start(bf16[128,2,2176]{2,1,0:T(2,128)(2,1)} %reshape.115), calls=%async_computation.2 | async-start | bytes 2228224 | tf_op jit(solution)/shard_map/all_to_all | solution.py:53
  209.2 55.4 %reduce-scatter.2.cloned.1.call-start = ((), (), s32[]{:S(2)}) async-start(), calls=%async_computation.5 | async-start | bytes 819200 | tf_op jit(solution)/shard_map/reduce_scatter | solution.py:68
Sparse Core Ops, SparseCore 0:
  10.1 32.8 all-gather.7
  45.0 47.1 all-gather.13
  94.3 45.0 all-gather.11
  141.3 45.0 all-gather.9
  246.1 18.4 reduce-scatter.1

commit v2 on v1

v2 whole, which is shorter than its diff:
```python
import functools

import jax
import jax.numpy as jnp
from jax import lax
from jax.experimental import pallas as pl
from jax.experimental.pallas import tpu as pltpu
from jax.sharding import PartitionSpec as P

F32, BF16 = jnp.float32, jnp.bfloat16
NT = (((1,), (1,)), ((), ()))


def kernel(
    ny,
    nz,
    ids,
    gates,
    scales,
    ck,
    og,
    wg,
    wu,
    wd,
    out,
    terms_out,
    raw,
    xd,
    hot,
    mix_hi,
    mix_lo,
    sendb,
    rows,
    w,
    psend,
    pin,
    keep,
    ret,
    came,
    fin32,
    fin16,
    fin_in,
    part_t,
    gather_t,
    loc_sem,
    a_send,
    a_recv,
    w_send,
    w_recv,
    d_send,
    d_recv,
    b_send,
    b_recv,
    p_send,
    p_recv,
    r_send,
    r_recv,
    f_send,
    f_recv,
    t_send,
    t_recv,
):
    n_chunk = keep.shape[0]
    per = ny // n_chunk
    cap = sendb.shape[3]
    half = sendb.shape[4]
    part = half // 2
    picks, tokens = ids.shape
    dp = lax.axis_index("dp")
    x = lax.axis_index("tensor")
    chip = lax.axis_index("expert")
    yy, zz = chip // nz, chip % nz
    h = x // 2
    a = (x + x // 2) % 2
    me = x % 2
    mate = 1 - me
    core = (dp + a) % 2
    a_peer = {"tensor": 2 * h + mate}
    b_peer = {"tensor": 3 - x}

    def turn(j):
        if ny == 8:
            return (j % 2) * 4 + ((j // 2) % 2) * 2 + j // 4
        return j

    def target(j, dz):
        return {"dp": core, "expert": ((yy + turn(j)) % ny) * nz + (zz + dz) % nz}

    def origin(j, dz):
        return {"dp": core, "expert": ((yy + ny - turn(j)) % ny) * nz + (zz + nz - dz) % nz}

    def for_all(j, dz, act):
        @pl.when((a == 1) | (j * nz + dz > 0))
        def _():
            act()

    weights = (wg, wu, wd)
    local = [
        pltpu.make_async_copy(ck, raw.at[me, 0], loc_sem.at[0]),
        pltpu.make_async_copy(og, raw.at[me, 1], loc_sem.at[1]),
    ]
    for m in range(3):
        for f in range(2):
            local.append(
                pltpu.make_async_copy(
                    weights[m].at[:, pl.ds(f * half, half)], w.at[m, me, f], loc_sem.at[2 + 2 * m + f]
                )
            )
    for copy in local:
        copy.start()

    barrier = pltpu.get_barrier_semaphore()
    for step in range(1, 4):
        pl.semaphore_signal(barrier, inc=1, device_id={"tensor": (x + step) % 4})

    def greet(j, carry):
        for dz in range(nz):
            for_all(j, dz, lambda: pl.semaphore_signal(barrier, inc=1, device_id=target(j, dz)))
        return carry

    lax.fori_loop(0, ny, greet, 0)

    r = lax.broadcasted_iota(jnp.int32, (ny * nz, tokens), 0)
    rj, rz = r // nz, r % nz
    expert = core * (ny * nz) + ((yy + turn(rj)) % ny) * nz + (zz + rz) % nz
    member = jnp.zeros((ny * nz, tokens), F32)
    gate = jnp.zeros((ny * nz, tokens), F32)
    for k in range(picks):
        same = ids[pl.ds(k, 1), :] == expert
        member = jnp.where(same, 1.0, member)
        gate = jnp.where(same, gates[pl.ds(k, 1), :], gate)
    before = lax.broadcasted_iota(jnp.int32, (tokens, tokens), 0) < lax.broadcasted_iota(
        jnp.int32, (tokens, tokens), 1
    )
    place = jnp.dot(member.astype(BF16), before.astype(F32).astype(BF16), preferred_element_type=F32)
    slot = lax.broadcasted_iota(jnp.int32, (ny * nz, cap, tokens), 1).astype(F32)
    place = jnp.where(member > 0.0, place, -1.0)
    pick = jnp.where(place[:, None, :] == slot, 1.0, 0.0)
    hot[...] = pick.reshape(ny, nz * cap, tokens).astype(BF16)
    mix = (pick * gate[:, None, :]).reshape(ny * nz * cap, tokens).T
    high = mix.astype(BF16)
    mix_hi[...] = high
    mix_lo[...] = (mix - high.astype(F32)).astype(BF16)

    pl.semaphore_wait(barrier, ny * nz + 2 + a)

    def remote(src, dst, send, recv, where):
        return pltpu.make_async_remote_copy(
            src_ref=src, dst_ref=dst, send_sem=send, recv_sem=recv, device_id=where
        )

    a_copies = [
        remote(ck, raw.at[me, 0], a_send.at[0], a_recv.at[0], a_peer),
        remote(og, raw.at[me, 1], a_send.at[1], a_recv.at[1], a_peer),
    ]
    for m in range(3):
        for f in range(2):
            a_copies.append(
                remote(
                    weights[m].at[:, pl.ds(f * half, half)],
                    w.at[m, me, f],
                    w_send.at[2 * m + f],
                    w_recv.at[2 * m + f],
                    a_peer,
                )
            )
    for copy in a_copies:
        copy.start()
    for i in range(2):
        local[i].wait()
    for i in range(2):
        remote(ck, raw.at[mate, i], a_send.at[i], a_recv.at[i], a_peer).wait_recv()

    for q in range(2):
        xd[q, 0] = (raw[q, 0].astype(F32) * scales[...]).astype(BF16)
        xd[q, 1] = raw[q, 1]

    def dispatch(j, carry):
        chosen = hot[j]
        for i in range(2):
            for q in range(2):
                got = jnp.dot(chosen, xd[q, i], preferred_element_type=F32)
                sendb[j, :, i, :, q * part : (q + 1) * part] = got.reshape(nz, cap, part).astype(BF16)
        for dz in range(nz):
            for_all(
                j,
                dz,
                lambda: remote(
                    sendb.at[j, dz], rows.at[h, j, dz], d_send.at[j], d_recv.at[j], target(j, dz)
                ).start(),
            )
        return carry

    lax.fori_loop(0, ny, dispatch, 0)

    @pl.when(a == 0)
    def _():
        rows[h, 0, 0] = sendb[0, 0]

    def all_but_own(j, ref, wait):
        @pl.when((a == 1) | (j > 0))
        def _():
            wait(ref)

        if nz > 1:

            @pl.when((a == 0) & (j == 0))
            def _():
                wait(ref.at[pl.ds(1, nz - 1)])

    def forward(j, carry):
        all_but_own(
            j,
            rows.at[h, j],
            lambda ref: remote(ref, ref, d_send.at[j], d_recv.at[j], b_peer).wait_recv(),
        )
        remote(rows.at[h, j], rows.at[h, j], b_send.at[j], b_recv.at[j], b_peer).start()
        return carry

    lax.fori_loop(0, ny, forward, 0)

    for i in range(2, 8):
        local[i].wait()
    for m in range(3):
        for f in range(2):
            remote(
                w.at[m, mate, f], w.at[m, mate, f], w_send.at[2 * m + f], w_recv.at[2 * m + f], a_peer
            ).wait_recv()

    n_rows = per * nz * cap

    def flat(ref):
        value = ref[...].astype(F32)
        return value.reshape(n_rows, value.shape[-1]).astype(BF16)

    def matrix(m, f):
        value = w[m, :, f]
        return value.reshape(2 * value.shape[1], half)

    def compute(c, carry):
        def arrived(i, carry):
            j = c * per + i
            other = rows.at[1 - h, j]
            remote(other, other, b_send.at[j], b_recv.at[j], b_peer).wait_recv()
            return carry

        lax.fori_loop(0, per, arrived, 0)
        first = c * per
        gate_pre = up_pre = back = 0.0
        for f in range(2):
            mine = flat(rows.at[f, pl.ds(first, per), :, 0])
            grad = flat(rows.at[f, pl.ds(first, per), :, 1])
            gate_pre += lax.dot_general(mine, matrix(0, f), NT, preferred_element_type=F32)
            up_pre += lax.dot_general(mine, matrix(1, f), NT, preferred_element_type=F32)
            back += lax.dot_general(grad, matrix(2, f), NT, preferred_element_type=F32)
        sigma = jax.nn.sigmoid(gate_pre)
        swish = gate_pre * sigma
        hidden = (swish * up_pre).astype(BF16)
        term = jnp.sum(hidden.astype(F32) * back, axis=1, keepdims=True)
        d_gate = (back * up_pre * sigma * (1.0 + gate_pre * (1.0 - sigma))).astype(BF16)
        d_up = (back * swish).astype(BF16)
        for which in range(2):
            f = h if which else 1 - h
            result = jnp.dot(d_gate, matrix(0, f), preferred_element_type=F32)
            result = result + jnp.dot(d_up, matrix(1, f), preferred_element_type=F32)
            if which:
                keep[c] = result
            else:
                psend[c] = result.astype(BF16)
                remote(psend.at[c], pin.at[c], p_send.at[c], p_recv.at[c], b_peer).start()
        wide = jnp.broadcast_to(term, (n_rows, 128)).reshape(per, nz, cap, 128).astype(BF16)
        ret[pl.ds(first, per), :, :, pl.ds(half, 128)] = wide
        return carry

    lax.fori_loop(0, n_chunk, compute, 0)

    def give_back(c, carry):
        first = c * per
        remote(psend.at[c], pin.at[c], p_send.at[c], p_recv.at[c], b_peer).wait_recv()
        total = keep[c] + pin[c].astype(F32)
        ret[pl.ds(first, per), :, :, pl.ds(0, half)] = total.reshape(per, nz, cap, half).astype(BF16)

        def one(i, carry):
            j = first + i
            for dz in range(nz):
                for_all(
                    j,
                    dz,
                    lambda: remote(
                        ret.at[j, dz], came.at[j, dz], r_send.at[j], r_recv.at[j], origin(j, dz)
                    ).start(),
                )
            return carry

        lax.fori_loop(0, per, one, 0)
        return carry

    lax.fori_loop(0, n_chunk, give_back, 0)

    @pl.when(a == 0)
    def _():
        came[0, 0] = ret[0, 0]

    def landed(j, carry):
        all_but_own(
            j,
            came.at[j],
            lambda ref: remote(ref, ref, r_send.at[j], r_recv.at[j], b_peer).wait_recv(),
        )
        return carry

    lax.fori_loop(0, ny, landed, 0)
    back_rows = came[:, :, :, pl.ds(0, half)].astype(F32).reshape(ny * nz * cap, half).astype(BF16)
    mixed = jnp.dot(mix_hi[...], back_rows, preferred_element_type=F32)
    mixed = mixed + jnp.dot(mix_lo[...], back_rows, preferred_element_type=F32)
    for q in range(2):
        fin32[q] = mixed[:, q * part : (q + 1) * part]
        fin16[q] = mixed[:, q * part : (q + 1) * part].astype(BF16)
    last = remote(fin16.at[mate], fin_in, f_send.at[0], f_recv.at[0], a_peer)
    last.start()

    seen = came[:, :, :, pl.ds(half, 128)].astype(F32).reshape(ny * nz, cap, 128)[:, :, :tokens]
    chosen = hot[...].astype(F32).reshape(ny * nz, cap, tokens)
    by_expert = jnp.sum(chosen * seen, axis=1)
    lines = []
    for k in range(picks):
        same = ids[pl.ds(k, 1), :] == expert
        lines.append(jnp.sum(jnp.where(same, by_expert, 0.0), axis=0, keepdims=True))
    own = jnp.concatenate(lines, axis=0)
    part_t[...] = own
    sends = []
    for step in range(1, 4):
        sends.append(
            remote(
                part_t,
                gather_t.at[step - 1],
                t_send.at[step - 1],
                t_recv.at[step - 1],
                {"tensor": (x + step) % 4},
            )
        )
        sends[-1].start()
    last.wait()
    out[...] = (fin32[me] + fin_in[...].astype(F32)).astype(BF16)
    for copy in sends:
        copy.wait()
    terms_out[...] = own + gather_t[0] + gather_t[1] + gather_t[2]

    for copy in a_copies:
        copy.wait_send()

    def drain(j, carry):
        all_but_own(
            j, sendb.at[j], lambda ref: remote(ref, ref, d_send.at[j], d_recv.at[j], b_peer).wait_send()
        )
        remote(rows.at[h, j], rows.at[h, j], b_send.at[j], b_recv.at[j], b_peer).wait_send()
        all_but_own(
            j, ret.at[j], lambda ref: remote(ref, ref, r_send.at[j], r_recv.at[j], b_peer).wait_send()
        )
        return carry

    lax.fori_loop(0, ny, drain, 0)
    for c in range(n_chunk):
        remote(psend.at[c], pin.at[c], p_send.at[c], p_recv.at[c], b_peer).wait_send()


def body(ny, nz, checkpoint, scales, out_grad, expert_ids, gates, w_gate, w_up, w_down):
    tokens, part = checkpoint.shape
    picks = expert_ids.shape[1]
    cap = tokens * picks // (2 * ny * nz)
    hidden = w_gate.shape[1]
    half = 2 * part
    n_chunk = 2
    n_rows = ny * nz * cap
    chunk = n_rows // n_chunk
    dma = pltpu.SemaphoreType.DMA
    vmem = pl.BlockSpec(memory_space=pltpu.VMEM)
    anyw = pl.BlockSpec(memory_space=pl.ANY)
    out, terms = pl.pallas_call(
        functools.partial(kernel, ny, nz),
        name="experts",
        out_shape=(
            jax.ShapeDtypeStruct((tokens, part), BF16),
            jax.ShapeDtypeStruct((picks, tokens), F32),
        ),
        in_specs=[vmem, vmem, vmem] + [anyw] * 5,
        out_specs=(vmem, vmem),
        scratch_shapes=[
            pltpu.VMEM((2, 2, tokens, part), BF16),
            pltpu.VMEM((2, 2, tokens, part), BF16),
            pltpu.VMEM((ny, nz * cap, tokens), BF16),
            pltpu.VMEM((tokens, n_rows), BF16),
            pltpu.VMEM((tokens, n_rows), BF16),
            pltpu.VMEM((ny, nz, 2, cap, half), BF16),
            pltpu.VMEM((2, ny, nz, 2, cap, half), BF16),
            pltpu.VMEM((3, 2, 2, hidden, half), BF16),
            pltpu.VMEM((n_chunk, chunk, half), BF16),
            pltpu.VMEM((n_chunk, chunk, half), BF16),
            pltpu.VMEM((n_chunk, chunk, half), F32),
            pltpu.VMEM((ny, nz, cap, half + 128), BF16),
            pltpu.VMEM((ny, nz, cap, half + 128), BF16),
            pltpu.VMEM((2, tokens, part), F32),
            pltpu.VMEM((2, tokens, part), BF16),
            pltpu.VMEM((tokens, part), BF16),
            pltpu.VMEM((picks, tokens), F32),
            pltpu.VMEM((3, picks, tokens), F32),
            dma((8,)),
            dma((2,)),
            dma((2,)),
            dma((6,)),
            dma((6,)),
            dma((ny,)),
            dma((ny,)),
            dma((ny,)),
            dma((ny,)),
            dma((n_chunk,)),
            dma((n_chunk,)),
            dma((ny,)),
            dma((ny,)),
            dma((1,)),
            dma((1,)),
            dma((3,)),
            dma((3,)),
        ],
        compiler_params=pltpu.CompilerParams(
            collective_id=0, has_side_effects=True, vmem_limit_bytes=60 * 1024 * 1024
        ),
    )(
        expert_ids.T,
        gates.T,
        scales[:, None],
        checkpoint,
        out_grad,
        w_gate[0],
        w_up[0],
        w_down[0],
    )
    return out, terms.T


def solution(mesh):
    n = mesh.shape["expert"]
    ny = 8 if n == 64 else n
    return jax.shard_map(
        functools.partial(body, ny, n // ny),
        mesh=mesh,
        in_specs=(
            P(("dp", "expert"), "tensor"),
            P(("dp", "expert")),
            P(("dp", "expert"), "tensor"),
            P(("dp", "expert"), None),
            P(("dp", "expert"), None),
            P(("dp", "expert"), "tensor", None),
            P(("dp", "expert"), "tensor", None),
            P(("dp", "expert"), "tensor", None),
        ),
        out_specs=(P(("dp", "expert"), "tensor"), P(("dp", "expert"), None)),
        check_vma=False,
    )
```

time: 276 us -> 171 us (0.62)
  waiting for transfers between devices: 190 us -> 0 us
  Pallas kernels: 0 us -> 167 us
  starting transfers between devices: 38.9 us -> 0 us
  matrix products: 15.4 us -> 0 us
  between operations: 14.1 us -> 0.66 us
  other arithmetic: 6.24 us -> 0 us
  local copies, waits for them, and re-layouts: 9.56 us -> 3.55 us
    pallas_call x0 -> x1, Pallas kernels: none -> 167 us  [body(): pl.pallas_call(functools.partial(kernel, ny, nz), name='experts', out_sha...]
    all_to_all x3 -> x0, waiting for transfers between devices: 92.2 us -> none  [the longest x1 32.3 us: body(): lax.all_to_all(packed.reshape(experts, own, width + 128), names, 0, 0, ti...]
    all_gather x4 -> x0, waiting for transfers between devices: 77.1 us -> none  [the longest x1 43.1 us: body(): wd = lax.all_gather(w_down[0], 'tensor', axis=0, tiled=True)]
    all_to_all x3 -> x0, starting transfers between devices: 38.7 us -> none  [the longest x1 16.7 us: body(): lax.all_to_all(send_x.reshape(experts, own, width), names, 0, 0, tiled=True)]
    reduce_scatter x1 -> x0, waiting for transfers between devices: 18.6 us -> none  [body(): lax.psum_scatter(joined, 'tensor', scatter_dimension=0, tiled=True)[0]]
    dot_general x10 -> x0, matrix products: 15.4 us -> none  [the longest x1 3.9 us: body(): up_pre = lax.dot_general(rows, wu, contract, preferred_element_type=f32)]
    reshape x7 -> x0, local copies, waits for them, and re-layouts: 5.83 us -> none  [the longest x1 1.5 us: body(): send_g.reshape(experts, own, width)]
  transfers between devices with their start and end apart: 8 -> 0, of which waited for: 7 -> 0; matrix products, arithmetic and copies ran while one was open for 5% -> 0% of each run, Pallas kernels for 0% -> 0%
where the time goes in v2:
time: 171 us
  Pallas kernels  167 us (98%)
  local copies, waits for them, and re-layouts  3.55 us (2%)
    pallas_call x1, Pallas kernels, body(): pl.pallas_call(functools.partial(kernel, ny, nz), name='experts', out_sha...  167 us

profile of v2, /device:TPU:1, one launch (start us, length us, event | category | flops | bytes accessed | tf_op | source)
XLA Modules:
  0.0 170.9 jit_solution(2388797757425173346)
XLA Ops:
  0.6 0.0 copy-start.1
  0.6 0.6 copy-done.1
  1.3 0.7 copy.10.scales
  2.0 166.7 %experts.1 = (bf16[128,512]{1,0:T(8,128)(2,1)}, f32[8,128]{1,0:T(8,128)}) custom-call(s32[8,128]{1,0:T(8,128)} %bitcast.10, f32[8,128]{1,0:T(8,128)} %bitcast.11, f32[128,1]{1,0:T(8,128)} %copy.10.scales, bf16[128,512]{1,0:T(8,128)(2,1)} %ck.1, bf16[128,512]{1,0:T(8,128)(2,1)} %og.1, bf16[192,2048]{1,0:T(8,128)(2,1)} %bitcast.7, bf16[192,2048]{1,0:T(8,128)(2,1)} %bitcast.8, ...), custom_call_target="tpu_custom_call" | custom-call | tf_op jit(solution)/shard_map/experts/pallas_call | solution.py:379
  168.7 0.0 copy-start
  168.8 1.6 copy.13
  170.3 0.0 copy-done
  170.3 0.6 copy.14
Async XLA Ops:
  0.6 0.7 copy-start.1
  168.7 1.6 copy-start

commit v3 on v2

v3 whole, which is shorter than its diff:
```python
import functools

import jax
import jax.numpy as jnp
from jax import lax
from jax.experimental import pallas as pl
from jax.experimental.pallas import tpu as pltpu
from jax.sharding import PartitionSpec as P

F32, BF16 = jnp.float32, jnp.bfloat16
NT = (((1,), (1,)), ((), ()))


def send_order(ny, nz):
    def far(step):
        return min(step[0], ny - step[0]) + min(step[1], nz - step[1])

    steps = sorted(((y, z) for y in range(ny) for z in range(nz)), key=far)
    order = []
    for y, z in steps:
        images = [(y, z), (-y, -z), (y, -z), (-y, z)]
        if ny == nz:
            images = [(y, z), (-y, -z), (z, -y), (-z, y), (y, -z), (-y, z), (z, y), (-z, -y)]
        for u, v in images:
            if (u % ny, v % nz) not in order:
                order.append((u % ny, v % nz))
    return order


def kernel(
    ny,
    nz,
    ids,
    gates,
    scales,
    ck,
    og,
    wg,
    wu,
    wd,
    out,
    terms_out,
    raw,
    hot,
    mix_hi,
    mix_lo,
    sendb,
    rows,
    w,
    psend,
    pin,
    keep,
    ret,
    came,
    fin32,
    fin16,
    fin_in,
    part_t,
    gather_t,
    loc_sem,
    a_send,
    a_recv,
    w_send,
    w_recv,
    d_send,
    d_recv,
    b_send,
    b_recv,
    p_send,
    p_recv,
    r_send,
    r_recv,
    f_send,
    f_recv,
    t_send,
    t_recv,
):
    order = send_order(ny, nz)
    peers = ny * nz
    groups = keep.shape[0]
    per = peers // groups
    cap, part = sendb.shape[3:]
    half = 2 * part
    picks, tokens = ids.shape
    dp = lax.axis_index("dp")
    x = lax.axis_index("tensor")
    chip = lax.axis_index("expert")
    yy, zz = chip // nz, chip % nz
    h = x // 2
    a = (x + x // 2) % 2
    me = x % 2
    mate = 1 - me
    core = (dp + a) % 2
    a_peer = {"tensor": 2 * h + mate}
    b_peer = {"tensor": 3 - x}
    to_y = [((yy + d) % ny) * nz for d in range(ny)]
    to_z = [(zz + d) % nz for d in range(nz)]

    def target(n):
        y, z = order[n]
        return {"dp": core, "expert": to_y[y] + to_z[z]}

    def origin(n):
        y, z = order[n]
        return {"dp": core, "expert": to_y[-y % ny] + to_z[-z % nz]}

    def each(first, count, act):
        for n in range(first, first + count):
            if n == 0:
                pl.when(a == 1)(functools.partial(act, n))
            else:
                act(n)

    def remote(src, dst, send, recv, where):
        return pltpu.make_async_remote_copy(
            src_ref=src, dst_ref=dst, send_sem=send, recv_sem=recv, device_id=where
        )

    def one_wait(g, ref, wait):
        @pl.when((a == 1) | (g > 0))
        def _():
            wait(ref.at[pl.ds(g * per, per)])

        if per > 1:

            @pl.when((a == 0) & (g == 0))
            def _():
                wait(ref.at[pl.ds(1, per - 1)])

    weights = (wg, wu, wd)
    local = [
        pltpu.make_async_copy(ck, raw.at[me, 0], loc_sem.at[0]),
        pltpu.make_async_copy(og, raw.at[me, 1], loc_sem.at[1]),
    ]
    for m in range(3):
        for f in range(2):
            local.append(
                pltpu.make_async_copy(
                    weights[m].at[:, pl.ds(f * half, half)], w.at[m, me, f], loc_sem.at[2 + 2 * m + f]
                )
            )
    for copy in local:
        copy.start()

    barrier = pltpu.get_barrier_semaphore()
    for step in range(1, 4):
        pl.semaphore_signal(barrier, inc=1, device_id={"tensor": (x + step) % 4})
    each(0, peers, lambda n: pl.semaphore_signal(barrier, inc=1, device_id=target(n)))

    r = lax.broadcasted_iota(jnp.int32, (peers, tokens), 0)
    expert = jnp.zeros((peers, tokens), jnp.int32)
    for n in range(peers):
        y, z = order[n]
        expert = jnp.where(r == n, core * peers + to_y[y] + to_z[z], expert)
    member = jnp.zeros((peers, tokens), F32)
    gate = jnp.zeros((peers, tokens), F32)
    for k in range(picks):
        same = ids[pl.ds(k, 1), :] == expert
        member = jnp.where(same, 1.0, member)
        gate = jnp.where(same, gates[pl.ds(k, 1), :], gate)
    before = lax.broadcasted_iota(jnp.int32, (tokens, tokens), 0) < lax.broadcasted_iota(
        jnp.int32, (tokens, tokens), 1
    )
    place = jnp.dot(member.astype(BF16), before.astype(F32).astype(BF16), preferred_element_type=F32)
    slot = lax.broadcasted_iota(jnp.int32, (peers, cap, tokens), 1).astype(F32)
    place = jnp.where(member > 0.0, place, -1.0)
    pick = jnp.where(place[:, None, :] == slot, 1.0, 0.0)
    hot[...] = pick.reshape(groups, per * cap, tokens).astype(BF16)
    mix = (pick * gate[:, None, :]).reshape(peers * cap, tokens).T
    high = mix.astype(BF16)
    mix_hi[...] = high
    mix_lo[...] = (mix - high.astype(F32)).astype(BF16)

    def build(q):
        sources = ((raw[q, 0].astype(F32) * scales[...]).astype(BF16), raw[q, 1])

        def group(g, carry):
            chosen = hot[g]
            for i in range(2):
                got = jnp.dot(chosen, sources[i], preferred_element_type=F32)
                sendb[q, pl.ds(g * per, per), i] = got.reshape(per, cap, part).astype(BF16)
            return carry

        lax.fori_loop(0, groups, group, 0)

        @pl.when(a == 0)
        def _():
            rows[2 * h + q, 0] = sendb[q, 0]

    def dispatch(q, turn):
        each(
            0,
            peers,
            lambda n: remote(
                sendb.at[q, n],
                rows.at[2 * h + q, n],
                d_send.at[turn, n // per],
                d_recv.at[turn, n // per],
                target(n),
            ).start(),
        )

    def forward(q, turn):
        def group(g, carry):
            one_wait(
                g,
                rows.at[2 * h + q],
                lambda ref: remote(ref, ref, d_send.at[turn, g], d_recv.at[turn, g], b_peer).wait_recv(),
            )
            ref = rows.at[2 * h + q, pl.ds(g * per, per)]
            remote(ref, ref, b_send.at[turn, g], b_recv.at[turn, g], b_peer).start()
            return carry

        lax.fori_loop(0, groups, group, 0)

    for i in range(2):
        local[i].wait()
    build(me)
    pl.semaphore_wait(barrier, peers + 2 + a)

    a_copies = [
        remote(ck, raw.at[me, 0], a_send.at[0], a_recv.at[0], a_peer),
        remote(og, raw.at[me, 1], a_send.at[1], a_recv.at[1], a_peer),
    ]
    for m in range(3):
        for f in range(2):
            a_copies.append(
                remote(
                    weights[m].at[:, pl.ds(f * half, half)],
                    w.at[m, me, f],
                    w_send.at[2 * m + f],
                    w_recv.at[2 * m + f],
                    a_peer,
                )
            )
    for copy in a_copies:
        copy.start()
    dispatch(me, 0)
    for i in range(2):
        remote(ck, raw.at[mate, i], a_send.at[i], a_recv.at[i], a_peer).wait_recv()
    build(mate)
    dispatch(mate, 1)
    forward(me, 0)
    forward(mate, 1)

    for i in range(2, 8):
        local[i].wait()
    for m in range(3):
        for f in range(2):
            remote(
                w.at[m, mate, f], w.at[m, mate, f], w_send.at[2 * m + f], w_recv.at[2 * m + f], a_peer
            ).wait_recv()

    wide = max(1, groups // 4)
    steps = groups // wide
    n_rows = wide * per * cap

    def give_back(g):
        remote(psend.at[g], pin.at[g], p_send.at[g], p_recv.at[g], b_peer).wait_recv()
        total = keep[g] + pin[g].astype(F32)
        ret[pl.ds(g * per, per), :, pl.ds(0, half)] = total.reshape(per, cap, half).astype(BF16)
        each(
            g * per,
            per,
            lambda n: remote(ret.at[n], came.at[n], r_send.at[g], r_recv.at[g], origin(n)).start(),
        )

    def compute(c, carry):
        first = c * wide
        for i in range(wide):
            other = rows.at[0, pl.ds((first + i) * per, per)]
            for turn in range(2):
                remote(
                    other, other, b_send.at[turn, first + i], b_recv.at[turn, first + i], b_peer
                ).wait_recv()
        gate_pre = up_pre = back = 0.0
        for fq in range(4):
            lanes = slice((fq % 2) * part, (fq % 2 + 1) * part)

            def matrix(m):
                value = w[m, :, fq // 2, :, lanes]
                return value.reshape(2 * value.shape[1], part)

            def flat(i):
                value = rows[fq, pl.ds(first * per, wide * per), i].astype(F32)
                return value.reshape(n_rows, part).astype(BF16)

            mine, grad = flat(0), flat(1)
            gate_pre += lax.dot_general(mine, matrix(0), NT, preferred_element_type=F32)
            up_pre += lax.dot_general(mine, matrix(1), NT, preferred_element_type=F32)
            back += lax.dot_general(grad, matrix(2), NT, preferred_element_type=F32)
        sigma = jax.nn.sigmoid(gate_pre)
        swish = gate_pre * sigma
        hidden = (swish * up_pre).astype(BF16)
        term = jnp.sum(hidden.astype(F32) * back, axis=1, keepdims=True)
        d_gate = (back * up_pre * sigma * (1.0 + gate_pre * (1.0 - sigma))).astype(BF16)
        d_up = (back * swish).astype(BF16)
        for own in range(2):
            f = h if own else 1 - h
            down_g, down_u = (w[m, :, f].reshape(2 * w.shape[3], half) for m in range(2))
            result = jnp.dot(d_gate, down_g, preferred_element_type=F32)
            result = result + jnp.dot(d_up, down_u, preferred_element_type=F32)
            result = result.reshape(wide, per * cap, half)
            if own:
                keep[pl.ds(first, wide)] = result
            else:
                psend[pl.ds(first, wide)] = result.astype(BF16)
                for i in range(wide):
                    g = first + i
                    remote(psend.at[g], pin.at[g], p_send.at[g], p_recv.at[g], b_peer).start()
        spread = jnp.broadcast_to(term, (n_rows, 128)).reshape(wide * per, cap, 128).astype(BF16)
        ret[pl.ds(first * per, wide * per), :, pl.ds(half, 128)] = spread
        for early in range(steps - 2):
            pl.when(c == early + 1)(functools.partial(give_back, early))
        return carry

    lax.fori_loop(0, steps, compute, 0)
    for g in range(max(0, steps - 2), groups):
        give_back(g)

    @pl.when(a == 0)
    def _():
        came[0] = ret[0]

    def landed(g, carry):
        one_wait(
            g, came, lambda ref: remote(ref, ref, r_send.at[g], r_recv.at[g], b_peer).wait_recv()
        )
        return carry

    lax.fori_loop(0, groups, landed, 0)
    back_rows = came[:, :, pl.ds(0, half)].astype(F32).reshape(peers * cap, half).astype(BF16)
    mixed = jnp.dot(mix_hi[...], back_rows, preferred_element_type=F32)
    mixed = mixed + jnp.dot(mix_lo[...], back_rows, preferred_element_type=F32)
    for q in range(2):
        fin32[q] = mixed[:, q * part : (q + 1) * part]
        fin16[q] = mixed[:, q * part : (q + 1) * part].astype(BF16)
    last = remote(fin16.at[mate], fin_in, f_send.at[0], f_recv.at[0], a_peer)
    last.start()

    seen = came[:, :, pl.ds(half, 128)].astype(F32)[:, :, :tokens]
    chosen = hot[...].astype(F32).reshape(peers, cap, tokens)
    by_expert = jnp.sum(chosen * seen, axis=1)
    lines = []
    for k in range(picks):
        same = ids[pl.ds(k, 1), :] == expert
        lines.append(jnp.sum(jnp.where(same, by_expert, 0.0), axis=0, keepdims=True))
    own = jnp.concatenate(lines, axis=0)
    part_t[...] = own
    sends = []
    for step in range(1, 4):
        sends.append(
            remote(
                part_t,
                gather_t.at[step - 1],
                t_send.at[step - 1],
                t_recv.at[step - 1],
                {"tensor": (x + step) % 4},
            )
        )
        sends[-1].start()
    last.wait()
    out[...] = (fin32[me] + fin_in[...].astype(F32)).astype(BF16)
    for copy in sends:
        copy.wait()
    terms_out[...] = own + gather_t[0] + gather_t[1] + gather_t[2]

    for copy in a_copies:
        copy.wait_send()

    def drain(g, carry):
        for turn, q in enumerate((me, mate)):
            one_wait(
                g,
                sendb.at[q],
                lambda ref: remote(ref, ref, d_send.at[turn, g], d_recv.at[turn, g], b_peer).wait_send(),
            )
            ref = rows.at[2 * h + q, pl.ds(g * per, per)]
            remote(ref, ref, b_send.at[turn, g], b_recv.at[turn, g], b_peer).wait_send()
        one_wait(
            g, ret, lambda ref: remote(ref, ref, r_send.at[g], r_recv.at[g], b_peer).wait_send()
        )
        remote(psend.at[g], pin.at[g], p_send.at[g], p_recv.at[g], b_peer).wait_send()
        return carry

    lax.fori_loop(0, groups, drain, 0)


def body(ny, nz, checkpoint, scales, out_grad, expert_ids, gates, w_gate, w_up, w_down):
    tokens, part = checkpoint.shape
    picks = expert_ids.shape[1]
    peers = ny * nz
    cap = tokens * picks // (2 * peers)
    hidden = w_gate.shape[1]
    half = 2 * part
    groups = max(2, peers // 8)
    group_rows = peers * cap // groups
    dma = pltpu.SemaphoreType.DMA
    vmem = pl.BlockSpec(memory_space=pltpu.VMEM)
    anyw = pl.BlockSpec(memory_space=pl.ANY)
    out, terms = pl.pallas_call(
        functools.partial(kernel, ny, nz),
        name="experts",
        out_shape=(
            jax.ShapeDtypeStruct((tokens, part), BF16),
            jax.ShapeDtypeStruct((picks, tokens), F32),
        ),
        in_specs=[vmem, vmem, vmem] + [anyw] * 5,
        out_specs=(vmem, vmem),
        scratch_shapes=[
            pltpu.VMEM((2, 2, tokens, part), BF16),
            pltpu.VMEM((groups, group_rows, tokens), BF16),
            pltpu.VMEM((tokens, peers * cap), BF16),
            pltpu.VMEM((tokens, peers * cap), BF16),
            pltpu.VMEM((2, peers, 2, cap, part), BF16),
            pltpu.VMEM((4, peers, 2, cap, part), BF16),
            pltpu.VMEM((3, 2, 2, hidden, half), BF16),
            pltpu.VMEM((groups, group_rows, half), BF16),
            pltpu.VMEM((groups, group_rows, half), BF16),
            pltpu.VMEM((groups, group_rows, half), F32),
            pltpu.VMEM((peers, cap, half + 128), BF16),
            pltpu.VMEM((peers, cap, half + 128), BF16),
            pltpu.VMEM((2, tokens, part), F32),
            pltpu.VMEM((2, tokens, part), BF16),
            pltpu.VMEM((tokens, part), BF16),
            pltpu.VMEM((picks, tokens), F32),
            pltpu.VMEM((3, picks, tokens), F32),
            dma((8,)),
            dma((2,)),
            dma((2,)),
            dma((6,)),
            dma((6,)),
            dma((2, groups)),
            dma((2, groups)),
            dma((2, groups)),
            dma((2, groups)),
            dma((groups,)),
            dma((groups,)),
            dma((groups,)),
            dma((groups,)),
            dma((1,)),
            dma((1,)),
            dma((3,)),
            dma((3,)),
        ],
        compiler_params=pltpu.CompilerParams(
            collective_id=0, has_side_effects=True, vmem_limit_bytes=60 * 1024 * 1024
        ),
    )(
        expert_ids.T,
        gates.T,
        scales[:, None],
        checkpoint,
        out_grad,
        w_gate[0],
        w_up[0],
        w_down[0],
    )
    return out, terms.T


def solution(mesh):
    n = mesh.shape["expert"]
    ny = 8 if n == 64 else n
    return jax.shard_map(
        functools.partial(body, ny, n // ny),
        mesh=mesh,
        in_specs=(
            P(("dp", "expert"), "tensor"),
            P(("dp", "expert")),
            P(("dp", "expert"), "tensor"),
            P(("dp", "expert"), None),
            P(("dp", "expert"), None),
            P(("dp", "expert"), "tensor", None),
            P(("dp", "expert"), "tensor", None),
            P(("dp", "expert"), "tensor", None),
        ),
        out_specs=(P(("dp", "expert"), "tensor"), P(("dp", "expert"), None)),
        check_vma=False,
    )
```

time: 171 us -> 132 us (0.77)
  the two profiles are of different devices: /device:TPU:1 before, /device:TPU:32 now
where the time goes in v3:
time: 132 us
  Pallas kernels  127 us (96%)
  local copies, waits for them, and re-layouts  3.55 us (3%)
    pallas_call x1, Pallas kernels, body(): pl.pallas_call(functools.partial(kernel, ny, nz), name='experts', out_sha...  127 us
    unnamed x6, local copies, waits for them, and re-layouts  2.81 us

profile of v3, /device:TPU:32, one launch (start us, length us, event | category | flops | bytes accessed | tf_op | source)
XLA Modules:
  0.0 131.7 jit_solution(15654393079790263054)
XLA Ops:
  0.6 0.0 copy-start.1
  0.6 0.6 copy-done.1
  1.3 0.7 copy.10.scales
  2.0 127.5 %experts.1 = (bf16[128,512]{1,0:T(8,128)(2,1)}, f32[8,128]{1,0:T(8,128)}) custom-call(s32[8,128]{1,0:T(8,128)} %bitcast.10, f32[8,128]{1,0:T(8,128)} %bitcast.11, f32[128,1]{1,0:T(8,128)} %copy.10.scales, bf16[128,512]{1,0:T(8,128)(2,1)} %ck.1, bf16[128,512]{1,0:T(8,128)(2,1)} %og.1, bf16[192,2048]{1,0:T(8,128)(2,1)} %bitcast.7, bf16[192,2048]{1,0:T(8,128)(2,1)} %bitcast.8, ...), custom_call_target="tpu_custom_call" | custom-call | tf_op jit(solution)/shard_map/experts/pallas_call | solution.py:401
  129.5 0.0 copy-start
  129.5 1.6 %copy.13 = bf16[128,512]{1,0:T(8,128)(2,1)} copy(bf16[128,512]{1,0:T(8,128)(2,1)} %get-tuple-element.8) | data formatting | bytes 262144
  131.1 0.0 copy-done
  131.1 0.6 copy.14
Async XLA Ops:
  0.6 0.7 copy-start.1
  129.5 1.6 %copy-start = (f32[8,128]{1,0:T(8,128)S(1)}, f32[8,128]{1,0:T(8,128)}, u32[]{:S(2)}) copy-start(f32[8,128]{1,0:T(8,128)} %get-tuple-element.5) | copy-start | bytes 12292

commit v4 on v3

v4 whole, which is shorter than its diff:
```python
import functools

import jax
import jax.numpy as jnp
from jax import lax
from jax.experimental import pallas as pl
from jax.experimental.pallas import tpu as pltpu
from jax.sharding import PartitionSpec as P

F32, BF16 = jnp.float32, jnp.bfloat16
NT = (((1,), (1,)), ((), ()))


def send_order(ny, nz):
    if (ny, nz) != (8, 8):
        return [(y, z) for y in range(ny) for z in range(nz)]

    def ring(u, v):
        images = []
        for y, z in ((u, v), (-u, -v), (v, -u), (-v, u)):
            if (y % ny, z % nz) not in images:
                images.append((y % ny, z % nz))
        return images

    return (
        (ring(0, 0) + ring(4, 4) + ring(0, 4) + ring(2, 2))
        + (ring(0, 1) + ring(3, 4))
        + (ring(0, 2) + ring(2, 4))
        + (ring(1, 1) + ring(3, 3))
        + (ring(0, 3) + ring(1, 4))
        + (ring(1, 2) + ring(2, 3))
        + (ring(1, -2) + ring(2, -3))
        + (ring(1, 3) + ring(1, -3))
    )


def kernel(
    ny,
    nz,
    ids,
    gates,
    scales,
    ck,
    og,
    wg,
    wu,
    wd,
    out,
    terms_out,
    raw,
    hot,
    mix_hi,
    mix_lo,
    sendb,
    rows,
    w,
    psend,
    pin,
    keep,
    other_part,
    term_part,
    pre,
    ret,
    came,
    term_half,
    term_in,
    term_ret,
    term_came,
    loc_sem,
    a_send,
    a_recv,
    w_send,
    w_recv,
    d_send,
    d_recv,
    b_send,
    b_recv,
    p_send,
    p_recv,
    r_send,
    r_recv,
    s_send,
    s_recv,
    t_send,
    t_recv,
    ready,
):
    order = send_order(ny, nz)
    peers = ny * nz
    groups = keep.shape[0]
    per = peers // groups
    cap, part = sendb.shape[3:]
    half = 2 * part
    picks, tokens = ids.shape
    dp = lax.axis_index("dp")
    x = lax.axis_index("tensor")
    chip = lax.axis_index("expert")
    yy, zz = chip // nz, chip % nz
    h = x // 2
    a = (x + x // 2) % 2
    me = x % 2
    mate = 1 - me
    core = (dp + a) % 2
    a_peer = {"tensor": 2 * h + mate}
    b_peer = {"tensor": 3 - x}
    cross_peer = {"tensor": 2 * h + mate, "dp": 1 - dp}
    to_y = [((yy + d) % ny) * nz for d in range(ny)]
    to_z = [(zz + d) % nz for d in range(nz)]

    def target(n):
        y, z = order[n]
        return {"dp": core, "expert": to_y[y] + to_z[z]}

    def origin(n, plane):
        y, z = order[n]
        return {"dp": core, "tensor": plane, "expert": to_y[-y % ny] + to_z[-z % nz]}

    def each(first, count, act):
        for n in range(first, first + count):
            if n == 0:
                pl.when(a == 1)(functools.partial(act, n))
            else:
                act(n)

    def remote(src, dst, send, recv, where):
        return pltpu.make_async_remote_copy(
            src_ref=src, dst_ref=dst, send_sem=send, recv_sem=recv, device_id=where
        )

    def one_wait(g, ref, wait):
        @pl.when((a == 1) | (g > 0))
        def _():
            wait(ref.at[pl.ds(g * per, per)])

        if per > 1:

            @pl.when((a == 0) & (g == 0))
            def _():
                wait(ref.at[pl.ds(1, per - 1)])

    weights = (wg, wu, wd)
    local = [
        pltpu.make_async_copy(ck, raw.at[me, 0], loc_sem.at[0]),
        pltpu.make_async_copy(og, raw.at[me, 1], loc_sem.at[1]),
    ]
    for m in range(3):
        for f in range(2):
            local.append(
                pltpu.make_async_copy(
                    weights[m].at[:, pl.ds(f * half, half)], w.at[m, me, f], loc_sem.at[2 + 2 * m + f]
                )
            )
    for copy in local:
        copy.start()

    barrier = pltpu.get_barrier_semaphore()
    for step in range(1, 4):
        pl.semaphore_signal(barrier, inc=1, device_id={"tensor": (x + step) % 4})
    pl.semaphore_signal(barrier, inc=1, device_id=cross_peer)
    each(0, peers, lambda n: pl.semaphore_signal(barrier, inc=1, device_id=target(n)))

    r = lax.broadcasted_iota(jnp.int32, (peers, tokens), 0)
    expert = jnp.zeros((peers, tokens), jnp.int32)
    for n in range(peers):
        y, z = order[n]
        expert = jnp.where(r == n, core * peers + to_y[y] + to_z[z], expert)
    before = lax.broadcasted_iota(jnp.int32, (tokens, tokens), 0) < lax.broadcasted_iota(
        jnp.int32, (tokens, tokens), 1
    )
    before = before.astype(F32).astype(BF16)
    slot = lax.broadcasted_iota(jnp.int32, (peers, cap, tokens), 1).astype(F32)
    experts = (expert, expert + (1 - 2 * core) * peers)

    def choose(side):
        member = jnp.zeros((peers, tokens), F32)
        gate = jnp.zeros((peers, tokens), F32)
        for k in range(picks):
            same = ids[pl.ds(k, 1), :] == experts[side]
            member = jnp.where(same, 1.0, member)
            gate = jnp.where(same, gates[pl.ds(k, 1), :], gate)
        place = jnp.dot(member.astype(BF16), before, preferred_element_type=F32)
        place = jnp.where(member > 0.0, place, -1.0)
        pick = jnp.where(place[:, None, :] == slot, 1.0, 0.0)
        hot[side] = pick.reshape(groups, per * cap, tokens).astype(BF16)
        mix = (pick * gate[:, None, :]).reshape(peers * cap, tokens).T
        high = mix.astype(BF16)
        mix_hi[side] = high
        mix_lo[side] = (mix - high.astype(F32)).astype(BF16)

    choose(0)
    diagonal = lax.broadcasted_iota(jnp.int32, (tokens, tokens), 0) == lax.broadcasted_iota(
        jnp.int32, (tokens, tokens), 1
    )
    scale = jnp.sum(jnp.where(diagonal, scales[...], 0.0), axis=1, keepdims=True)

    def build(q):
        sources = ((raw[q, 0].astype(F32) * scale).astype(BF16), raw[q, 1])

        def group(g, carry):
            chosen = hot[0, g]
            for i in range(2):
                got = jnp.dot(chosen, sources[i], preferred_element_type=F32)
                sendb[q, pl.ds(g * per, per), i] = got.reshape(per, cap, part).astype(BF16)
            return carry

        lax.fori_loop(0, groups, group, 0)

        @pl.when(a == 0)
        def _():
            rows[2 * h + q, 0] = sendb[q, 0]

    def dispatch(q, turn):
        each(
            0,
            peers,
            lambda n: remote(
                sendb.at[q, n],
                rows.at[2 * h + q, n],
                d_send.at[turn, n // per],
                d_recv.at[turn, n // per],
                target(n),
            ).start(),
        )

    def forward(q, turn, g):
        one_wait(
            g,
            rows.at[2 * h + q],
            lambda ref: remote(ref, ref, d_send.at[turn, g], d_recv.at[turn, g], b_peer).wait_recv(),
        )
        ref = rows.at[2 * h + q, pl.ds(g * per, per)]
        remote(ref, ref, b_send.at[turn, g], b_recv.at[turn, g], b_peer).start()

    for i in range(2):
        local[i].wait()
    build(me)
    pl.semaphore_wait(barrier, peers + 3 + a)
    pl.semaphore_signal(ready, inc=1, device_id=cross_peer)

    a_copies = [
        remote(ck, raw.at[me, 0], a_send.at[0], a_recv.at[0], a_peer),
        remote(og, raw.at[me, 1], a_send.at[1], a_recv.at[1], a_peer),
    ]
    for m in range(3):
        for f in range(2):
            a_copies.append(
                remote(
                    weights[m].at[:, pl.ds(f * half, half)],
                    w.at[m, me, f],
                    w_send.at[2 * m + f],
                    w_recv.at[2 * m + f],
                    a_peer,
                )
            )
    for copy in a_copies:
        copy.start()
    dispatch(me, 0)
    choose(1)
    for i in range(2):
        remote(ck, raw.at[mate, i], a_send.at[i], a_recv.at[i], a_peer).wait_recv()
    build(mate)
    dispatch(mate, 1)
    small = max(1, groups // 4)

    def product(first, count, i, m, q):
        total = 0.0
        for fq in range(4):
            lanes = slice((fq % 2) * part, (fq % 2 + 1) * part)
            value = rows[fq, pl.ds(first * per, count * per), i].astype(F32)
            value = value.reshape(count * per * cap, part).astype(BF16)
            total += lax.dot_general(
                value, w[m, q, fq // 2, :, lanes], NT, preferred_element_type=F32
            )
        return total

    def grads(gate_pre, up_pre, back):
        sigma = jax.nn.sigmoid(gate_pre)
        swish = gate_pre * sigma
        hidden = (swish * up_pre).astype(BF16)
        term = jnp.sum(hidden.astype(F32) * back, axis=1, keepdims=True)
        d_gate = (back * up_pre * sigma * (1.0 + gate_pre * (1.0 - sigma))).astype(BF16)
        d_up = (back * swish).astype(BF16)
        return term, d_gate, d_up

    def results(d_gate, d_up, q, f, count):
        result = jnp.dot(d_gate, w[0, q, f], preferred_element_type=F32)
        result = result + jnp.dot(d_up, w[1, q, f], preferred_element_type=F32)
        return result.reshape(count, per * cap, half)

    def weight_landed(m):
        for f in range(2):
            remote(
                w.at[m, mate, f], w.at[m, mate, f], w_send.at[2 * m + f], w_recv.at[2 * m + f], a_peer
            ).wait_recv()

    def early(first, count, m):
        value = product(first, count, 0, m, mate)
        pre[m, pl.ds(first, count)] = value.reshape(count, per * cap, value.shape[-1])

    def own_quarter(c):
        first = c * small
        for i in range(small):
            other = rows.at[0, pl.ds((first + i) * per, per)]
            for turn in range(2):
                remote(
                    other, other, b_send.at[turn, first + i], b_recv.at[turn, first + i], b_peer
                ).wait_recv()
        term, d_gate, d_up = grads(
            product(first, small, 0, 0, me), product(first, small, 0, 1, me), product(first, small, 1, 2, me)
        )
        where = pl.ds(first, small)
        other_part[where] = results(d_gate, d_up, me, 1 - h, small)
        keep[where] = results(d_gate, d_up, me, h, small)
        n_rows = small * per * cap
        term_part[where] = jnp.broadcast_to(term, (n_rows, 128)).reshape(small, per * cap, 128)
        early(first, small, 0)

    def forward_own(g, carry):
        forward(me, 0, g)
        return carry

    lax.fori_loop(0, groups, forward_own, 0)
    for i in range(2, 8):
        local[i].wait()
    weight_landed(0)
    steps = groups // small

    def forward_mate(c, carry):
        @pl.when(c < steps)
        def _():
            for i in range(small):
                forward(mate, 1, c * small + i)

        @pl.when(c == steps)
        def _():
            weight_landed(1)
            for k in range(steps - 1):
                early(k * small, small, 1)

        @pl.when(c > 0)
        def _():
            own_quarter(c - 1)

        return carry

    lax.fori_loop(0, steps + 1, forward_mate, 0)
    early((steps - 1) * small, small, 1)
    weight_landed(2)

    def give_back(g):
        remote(psend.at[g], pin.at[g], p_send.at[g], p_recv.at[g], b_peer).wait_recv()
        remote(term_half.at[g], term_in.at[g], t_send.at[g], t_recv.at[g], b_peer).wait_recv()
        total = (keep[g] + pin[g].astype(F32)).reshape(per, cap, half).astype(BF16)
        where = pl.ds(g * per, per)
        for q in range(2):
            ret[q, where] = total[:, :, q * part : (q + 1) * part]
        term_ret[where] = (term_half[g] + term_in[g])[:, None, :]

        def send(side, n):
            q, plane = ((me, x), (mate, 2 * h + mate))[side]
            to = origin(n, plane)
            remote(ret.at[q, n], came.at[side, n], r_send.at[side, g], r_recv.at[side, g], to).start()
            remote(
                term_ret.at[n], term_came.at[side, n], s_send.at[side, g], s_recv.at[side, g], to
            ).start()

        for n in range(g * per, g * per + per):
            send(1, n)
            each(n, 1, functools.partial(send, 0))

    def mate_quarter(c, carry):
        first = c * small
        where = pl.ds(first, small)
        n_rows = small * per * cap
        term, d_gate, d_up = grads(
            pre[0, where].reshape(n_rows, -1),
            pre[1, where].reshape(n_rows, -1),
            product(first, small, 1, 2, mate),
        )
        psend[where] = (other_part[where] + results(d_gate, d_up, mate, 1 - h, small)).astype(BF16)
        for i in range(small):
            g = first + i
            remote(psend.at[g], pin.at[g], p_send.at[g], p_recv.at[g], b_peer).start()
        keep[where] = keep[where] + results(d_gate, d_up, mate, h, small)
        term = term_part[where].reshape(n_rows, 128) + term
        lane = lax.broadcasted_iota(jnp.int32, (small * per, cap, 128), 2)
        at = lax.broadcasted_iota(jnp.int32, (small * per, cap, 128), 1)
        line = jnp.sum(jnp.where(lane == at, term.reshape(small * per, cap, 128), 0.0), axis=1)
        term_half[where] = line.reshape(small, per, 128)
        for i in range(small):
            g = first + i
            remote(term_half.at[g], term_in.at[g], t_send.at[g], t_recv.at[g], b_peer).start()
        return carry

    lax.fori_loop(0, steps, mate_quarter, 0)
    pl.semaphore_wait(ready, 1)
    for g in range(groups):
        give_back(g)

    @pl.when(a == 0)
    def _():
        came[0, 0] = ret[me, 0]
        term_came[0, 0] = term_ret[0]

    def returned(g, ref, side, sends, recvs):
        act = lambda ref: remote(ref, ref, sends.at[side, g], recvs.at[side, g], b_peer).wait_recv()
        if side == 0:
            one_wait(g, ref.at[0], act)
        else:
            act(ref.at[1, pl.ds(g * per, per)])

    def landed(g, carry):
        for side in range(2):
            returned(g, came, side, r_send, r_recv)
            returned(g, term_came, side, s_send, s_recv)
        return carry

    lax.fori_loop(0, groups, landed, 0)
    mixed = 0.0
    for side in range(2):
        back_rows = came[side].astype(F32).reshape(peers * cap, part).astype(BF16)
        mixed += jnp.dot(mix_hi[side], back_rows, preferred_element_type=F32)
        mixed += jnp.dot(mix_lo[side], back_rows, preferred_element_type=F32)
    out[...] = mixed.astype(BF16)

    lane = lax.broadcasted_iota(jnp.int32, (peers, cap, 128), 2)
    at = lax.broadcasted_iota(jnp.int32, (peers, cap, 128), 1)
    by_expert = []
    for side in range(2):
        line = term_came[side].reshape(peers, 128)
        seen = jnp.sum(jnp.where(lane == at, line[:, None, :], 0.0), axis=2, keepdims=True)
        chosen = hot[side].astype(F32).reshape(peers, cap, tokens)
        by_expert.append(jnp.sum(chosen * seen, axis=1))
    for k in range(picks):
        total = 0.0
        for side in range(2):
            same = ids[pl.ds(k, 1), :] == experts[side]
            total += jnp.sum(jnp.where(same, by_expert[side], 0.0), axis=0, keepdims=True)
        terms_out[pl.ds(k, 1), :] = total

    for copy in a_copies:
        copy.wait_send()

    def drain(g, carry):
        for turn, q in enumerate((me, mate)):
            one_wait(
                g,
                sendb.at[q],
                lambda ref: remote(ref, ref, d_send.at[turn, g], d_recv.at[turn, g], b_peer).wait_send(),
            )
            ref = rows.at[2 * h + q, pl.ds(g * per, per)]
            remote(ref, ref, b_send.at[turn, g], b_recv.at[turn, g], b_peer).wait_send()
        for side, q in enumerate((me, mate)):
            if side == 0:
                one_wait(
                    g,
                    ret.at[q],
                    lambda ref: remote(ref, ref, r_send.at[0, g], r_recv.at[0, g], b_peer).wait_send(),
                )
                one_wait(
                    g,
                    term_ret,
                    lambda ref: remote(ref, ref, s_send.at[0, g], s_recv.at[0, g], b_peer).wait_send(),
                )
            else:
                for ref, sends, recvs in ((ret.at[q], r_send, r_recv), (term_ret, s_send, s_recv)):
                    ref = ref.at[pl.ds(g * per, per)]
                    remote(ref, ref, sends.at[1, g], recvs.at[1, g], b_peer).wait_send()
        remote(term_half.at[g], term_in.at[g], t_send.at[g], t_recv.at[g], b_peer).wait_send()
        remote(psend.at[g], pin.at[g], p_send.at[g], p_recv.at[g], b_peer).wait_send()
        return carry

    lax.fori_loop(0, groups, drain, 0)


def body(ny, nz, checkpoint, scales, out_grad, expert_ids, gates, w_gate, w_up, w_down):
    tokens, part = checkpoint.shape
    picks = expert_ids.shape[1]
    peers = ny * nz
    cap = tokens * picks // (2 * peers)
    hidden = w_gate.shape[1]
    half = 2 * part
    groups = max(2, peers // 8)
    group_rows = peers * cap // groups
    dma = pltpu.SemaphoreType.DMA
    vmem = pl.BlockSpec(memory_space=pltpu.VMEM)
    anyw = pl.BlockSpec(memory_space=pl.ANY)
    out, terms = pl.pallas_call(
        functools.partial(kernel, ny, nz),
        name="experts",
        out_shape=(
            jax.ShapeDtypeStruct((tokens, part), BF16),
            jax.ShapeDtypeStruct((picks, tokens), F32),
        ),
        in_specs=[vmem, vmem, vmem] + [anyw] * 5,
        out_specs=(vmem, vmem),
        scratch_shapes=[
            pltpu.VMEM((2, 2, tokens, part), BF16),
            pltpu.VMEM((2, groups, group_rows, tokens), BF16),
            pltpu.VMEM((2, tokens, peers * cap), BF16),
            pltpu.VMEM((2, tokens, peers * cap), BF16),
            pltpu.VMEM((2, peers, 2, cap, part), BF16),
            pltpu.VMEM((4, peers, 2, cap, part), BF16),
            pltpu.VMEM((3, 2, 2, hidden, half), BF16),
            pltpu.VMEM((groups, group_rows, half), BF16),
            pltpu.VMEM((groups, group_rows, half), BF16),
            pltpu.VMEM((groups, group_rows, half), F32),
            pltpu.VMEM((groups, group_rows, half), F32),
            pltpu.VMEM((groups, group_rows, 128), F32),
            pltpu.VMEM((2, groups, group_rows, hidden), F32),
            pltpu.VMEM((2, peers, cap, part), BF16),
            pltpu.VMEM((2, peers, cap, part), BF16),
            pltpu.VMEM((groups, peers // groups, 128), F32),
            pltpu.VMEM((groups, peers // groups, 128), F32),
            pltpu.VMEM((peers, 1, 128), F32),
            pltpu.VMEM((2, peers, 1, 128), F32),
            dma((8,)),
            dma((2,)),
            dma((2,)),
            dma((6,)),
            dma((6,)),
            dma((2, groups)),
            dma((2, groups)),
            dma((2, groups)),
            dma((2, groups)),
            dma((groups,)),
            dma((groups,)),
            dma((2, groups)),
            dma((2, groups)),
            dma((2, groups)),
            dma((2, groups)),
            dma((groups,)),
            dma((groups,)),
            pltpu.SemaphoreType.REGULAR,
        ],
        compiler_params=pltpu.CompilerParams(
            collective_id=0, has_side_effects=True, vmem_limit_bytes=60 * 1024 * 1024
        ),
    )(
        expert_ids.T,
        gates.T,
        scales[None, :],
        checkpoint,
        out_grad,
        w_gate[0],
        w_up[0],
        w_down[0],
    )
    return out, terms.T


def solution(mesh):
    n = mesh.shape["expert"]
    ny = 8 if n == 64 else n
    return jax.shard_map(
        functools.partial(body, ny, n // ny),
        mesh=mesh,
        in_specs=(
            P(("dp", "expert"), "tensor"),
            P(("dp", "expert")),
            P(("dp", "expert"), "tensor"),
            P(("dp", "expert"), None),
            P(("dp", "expert"), None),
            P(("dp", "expert"), "tensor", None),
            P(("dp", "expert"), "tensor", None),
            P(("dp", "expert"), "tensor", None),
        ),
        out_specs=(P(("dp", "expert"), "tensor"), P(("dp", "expert"), None)),
        check_vma=False,
    )
```

time: 132 us -> 125 us (0.947)
  the two profiles are of different devices: /device:TPU:32 before, /device:TPU:1 now
where the time goes in v4:
time: 125 us
  Pallas kernels  122 us (98%)
  local copies, waits for them, and re-layouts  2.17 us (2%)
    pallas_call x1, Pallas kernels, body(): pl.pallas_call(functools.partial(kernel, ny, nz), name='experts', out_sha...  122 us

profile of v4, /device:TPU:1, one launch (start us, length us, event | category | flops | bytes accessed | tf_op | source)
XLA Modules:
  0.0 124.9 jit_solution(17409432135918260204)
XLA Ops:
  0.6 122.1 %experts.1 = (bf16[128,512]{1,0:T(8,128)(2,1)}, f32[8,128]{1,0:T(8,128)}) custom-call(s32[8,128]{1,0:T(8,128)} %bitcast.10, f32[8,128]{1,0:T(8,128)} %bitcast.11, f32[1,128]{1,0:T(1,128)} %bitcast.13, bf16[128,512]{1,0:T(8,128)(2,1)} %ck.1, bf16[128,512]{1,0:T(8,128)(2,1)} %og.1, bf16[192,2048]{1,0:T(8,128)(2,1)} %bitcast.7, bf16[192,2048]{1,0:T(8,128)(2,1)} %bitcast.8, ...), custom_call_target="tpu_custom_call" | custom-call | tf_op jit(solution)/shard_map/experts/pallas_call | solution.py:488
  122.7 0.0 copy-start
  122.7 1.6 %copy.12 = bf16[128,512]{1,0:T(8,128)(2,1)} copy(bf16[128,512]{1,0:T(8,128)(2,1)} %get-tuple-element.8) | data formatting | bytes 262144
  124.3 0.0 copy-done
  124.3 0.6 copy.13
Async XLA Ops:
  122.7 1.6 %copy-start = (f32[8,128]{1,0:T(8,128)S(1)}, f32[8,128]{1,0:T(8,128)}, u32[]{:S(2)}) copy-start(f32[8,128]{1,0:T(8,128)} %get-tuple-element.5) | copy-start | bytes 12292

commit v5 on v4

--- a/solution.py
+++ b/solution.py
@@ -83,11 +83,15 @@
     s_recv,
     t_send,
     t_recv,
+    c_send,
+    c_recv,
+    k_send,
+    k_recv,
     ready,
 ):
     order = send_order(ny, nz)
     peers = ny * nz
-    groups = keep.shape[0]
+    groups = keep.shape[1]
     per = peers // groups
     cap, part = sendb.shape[3:]
     half = 2 * part
@@ -102,25 +106,25 @@
     mate = 1 - me
     core = (dp + a) % 2
     a_peer = {"tensor": 2 * h + mate}
-    b_peer = {"tensor": 3 - x}
-    cross_peer = {"tensor": 2 * h + mate, "dp": 1 - dp}
+    b_peer = {"tensor": 3 - x, "dp": core}
+    sibling = {"dp": 1 - dp}
     to_y = [((yy + d) % ny) * nz for d in range(ny)]
     to_z = [(zz + d) % nz for d in range(nz)]
 
     def target(n):
         y, z = order[n]
-        return {"dp": core, "expert": to_y[y] + to_z[z]}
+        return {"expert": to_y[y] + to_z[z]}
 
     def origin(n, plane):
         y, z = order[n]
-        return {"dp": core, "tensor": plane, "expert": to_y[-y % ny] + to_z[-z % nz]}
+        return {"tensor": plane, "expert": to_y[-y % ny] + to_z[-z % nz]}
+
+    def landing(q):
+        return (1 - a) * (2 * h + q) + a * (4 + q)
 
     def each(first, count, act):
-        for n in range(first, first + count):
-            if n == 0:
-                pl.when(a == 1)(functools.partial(act, n))
-            else:
-                act(n)
+        for n in range(max(first, 1), first + count):
+            act(n)
 
     def remote(src, dst, send, recv, where):
         return pltpu.make_async_remote_copy(
@@ -128,13 +132,13 @@
         )
 
     def one_wait(g, ref, wait):
-        @pl.when((a == 1) | (g > 0))
+        @pl.when(g > 0)
         def _():
             wait(ref.at[pl.ds(g * per, per)])
 
         if per > 1:
 
-            @pl.when((a == 0) & (g == 0))
+            @pl.when(g == 0)
             def _():
                 wait(ref.at[pl.ds(1, per - 1)])
 
@@ -156,7 +160,8 @@
     barrier = pltpu.get_barrier_semaphore()
     for step in range(1, 4):
         pl.semaphore_signal(barrier, inc=1, device_id={"tensor": (x + step) % 4})
-    pl.semaphore_signal(barrier, inc=1, device_id=cross_peer)
+    pl.semaphore_signal(barrier, inc=1, device_id=sibling)
+    pl.semaphore_signal(barrier, inc=1, device_id={"tensor": 3 - x, "dp": 1 - dp})
     each(0, peers, lambda n: pl.semaphore_signal(barrier, inc=1, device_id=target(n)))
 
     r = lax.broadcasted_iota(jnp.int32, (peers, tokens), 0)
@@ -205,9 +210,7 @@
 
         lax.fori_loop(0, groups, group, 0)
 
-        @pl.when(a == 0)
-        def _():
-            rows[2 * h + q, 0] = sendb[q, 0]
+        rows[landing(q), 0] = sendb[q, 0]
 
     def dispatch(q, turn):
         each(
@@ -215,7 +218,7 @@
             peers,
             lambda n: remote(
                 sendb.at[q, n],
-                rows.at[2 * h + q, n],
+                rows.at[landing(q), n],
                 d_send.at[turn, n // per],
                 d_recv.at[turn, n // per],
                 target(n),
@@ -225,17 +228,22 @@
     def forward(q, turn, g):
         one_wait(
             g,
-            rows.at[2 * h + q],
+            rows.at[landing(q)],
             lambda ref: remote(ref, ref, d_send.at[turn, g], d_recv.at[turn, g], b_peer).wait_recv(),
         )
-        ref = rows.at[2 * h + q, pl.ds(g * per, per)]
-        remote(ref, ref, b_send.at[turn, g], b_recv.at[turn, g], b_peer).start()
+        ref = rows.at[landing(q), pl.ds(g * per, per)]
+        place = rows.at[2 * h + q, pl.ds(g * per, per)]
+        remote(ref, place, b_send.at[turn, g], b_recv.at[turn, g], b_peer).start()
+
+        @pl.when(a == 1)
+        def _():
+            remote(ref, place, c_send.at[turn, g], c_recv.at[turn, g], sibling).start()
 
     for i in range(2):
         local[i].wait()
     build(me)
-    pl.semaphore_wait(barrier, peers + 3 + a)
-    pl.semaphore_signal(ready, inc=1, device_id=cross_peer)
+    pl.semaphore_wait(barrier, peers + 4)
+    pl.semaphore_signal(ready, inc=1, device_id=a_peer)
 
     a_copies = [
         remote(ck, raw.at[me, 0], a_send.at[0], a_recv.at[0], a_peer),
@@ -302,15 +310,18 @@
         for i in range(small):
             other = rows.at[0, pl.ds((first + i) * per, per)]
             for turn in range(2):
-                remote(
-                    other, other, b_send.at[turn, first + i], b_recv.at[turn, first + i], b_peer
-                ).wait_recv()
+                g = first + i
+                remote(other, other, b_send.at[turn, g], b_recv.at[turn, g], b_peer).wait_recv()
+
+                @pl.when(a == 1)
+                def _():
+                    remote(other, other, c_send.at[turn, g], c_recv.at[turn, g], sibling).wait_recv()
         term, d_gate, d_up = grads(
             product(first, small, 0, 0, me), product(first, small, 0, 1, me), product(first, small, 1, 2, me)
         )
         where = pl.ds(first, small)
         other_part[where] = results(d_gate, d_up, me, 1 - h, small)
-        keep[where] = results(d_gate, d_up, me, h, small)
+        keep[0, where] = results(d_gate, d_up, me, h, small)
         n_rows = small * per * cap
         term_part[where] = jnp.broadcast_to(term, (n_rows, 128)).reshape(small, per * cap, 128)
         early(first, small, 0)
@@ -347,14 +358,25 @@
     early((steps - 1) * small, small, 1)
     weight_landed(2)
 
+    def to_sibling(g):
+        return (
+            remote(keep.at[0, g], keep.at[1, g], k_send.at[0, g], k_recv.at[0, g], sibling),
+            remote(term_half.at[0, g], term_half.at[1, g], k_send.at[1, g], k_recv.at[1, g], sibling),
+        )
+
     def give_back(g):
+        @pl.when(a == 1)
+        def _():
+            for copy in to_sibling(g):
+                copy.wait_recv()
+
         remote(psend.at[g], pin.at[g], p_send.at[g], p_recv.at[g], b_peer).wait_recv()
-        remote(term_half.at[g], term_in.at[g], t_send.at[g], t_recv.at[g], b_peer).wait_recv()
-        total = (keep[g] + pin[g].astype(F32)).reshape(per, cap, half).astype(BF16)
+        remote(term_half.at[0, g], term_in.at[g], t_send.at[g], t_recv.at[g], b_peer).wait_recv()
+        total = (keep[a, g] + pin[g].astype(F32)).reshape(per, cap, half).astype(BF16)
         where = pl.ds(g * per, per)
         for q in range(2):
             ret[q, where] = total[:, :, q * part : (q + 1) * part]
-        term_ret[where] = (term_half[g] + term_in[g])[:, None, :]
+        term_ret[where] = (term_half[a, g] + term_in[g])[:, None, :]
 
         def send(side, n):
             q, plane = ((me, x), (mate, 2 * h + mate))[side]
@@ -381,15 +403,20 @@
         for i in range(small):
             g = first + i
             remote(psend.at[g], pin.at[g], p_send.at[g], p_recv.at[g], b_peer).start()
-        keep[where] = keep[where] + results(d_gate, d_up, mate, h, small)
+        keep[0, where] = keep[0, where] + results(d_gate, d_up, mate, h, small)
         term = term_part[where].reshape(n_rows, 128) + term
         lane = lax.broadcasted_iota(jnp.int32, (small * per, cap, 128), 2)
         at = lax.broadcasted_iota(jnp.int32, (small * per, cap, 128), 1)
         line = jnp.sum(jnp.where(lane == at, term.reshape(small * per, cap, 128), 0.0), axis=1)
-        term_half[where] = line.reshape(small, per, 128)
+        term_half[0, where] = line.reshape(small, per, 128)
         for i in range(small):
             g = first + i
-            remote(term_half.at[g], term_in.at[g], t_send.at[g], t_recv.at[g], b_peer).start()
+            remote(term_half.at[0, g], term_in.at[g], t_send.at[g], t_recv.at[g], b_peer).start()
+
+            @pl.when(a == 1)
+            def _():
+                for copy in to_sibling(g):
+                    copy.start()
         return carry
 
     lax.fori_loop(0, steps, mate_quarter, 0)
@@ -397,10 +424,8 @@
     for g in range(groups):
         give_back(g)
 
-    @pl.when(a == 0)
-    def _():
-        came[0, 0] = ret[me, 0]
-        term_came[0, 0] = term_ret[0]
+    came[0, 0] = ret[me, 0]
+    term_came[0, 0] = term_ret[0]
 
     def returned(g, ref, side, sends, recvs):
         act = lambda ref: remote(ref, ref, sends.at[side, g], recvs.at[side, g], b_peer).wait_recv()
@@ -448,8 +473,13 @@
                 sendb.at[q],
                 lambda ref: remote(ref, ref, d_send.at[turn, g], d_recv.at[turn, g], b_peer).wait_send(),
             )
-            ref = rows.at[2 * h + q, pl.ds(g * per, per)]
+            ref = rows.at[landing(q), pl.ds(g * per, per)]
             remote(ref, ref, b_send.at[turn, g], b_recv.at[turn, g], b_peer).wait_send()
+
+            @pl.when(a == 1)
+            def _():
+                remote(ref, ref, c_send.at[turn, g], c_recv.at[turn, g], sibling).wait_send()
+
         for side, q in enumerate((me, mate)):
             if side == 0:
                 one_wait(
@@ -466,7 +496,13 @@
                 for ref, sends, recvs in ((ret.at[q], r_send, r_recv), (term_ret, s_send, s_recv)):
                     ref = ref.at[pl.ds(g * per, per)]
                     remote(ref, ref, sends.at[1, g], recvs.at[1, g], b_peer).wait_send()
-        remote(term_half.at[g], term_in.at[g], t_send.at[g], t_recv.at[g], b_peer).wait_send()
+        remote(term_half.at[0, g], term_in.at[g], t_send.at[g], t_recv.at[g], b_peer).wait_send()
+
+        @pl.when(a == 1)
+        def _():
+            for copy in to_sibling(g):
+                copy.wait_send()
+
         remote(psend.at[g], pin.at[g], p_send.at[g], p_recv.at[g], b_peer).wait_send()
         return carry
 
@@ -500,17 +536,17 @@
             pltpu.VMEM((2, tokens, peers * cap), BF16),
             pltpu.VMEM((2, tokens, peers * cap), BF16),
             pltpu.VMEM((2, peers, 2, cap, part), BF16),
-            pltpu.VMEM((4, peers, 2, cap, part), BF16),
+            pltpu.VMEM((6, peers, 2, cap, part), BF16),
             pltpu.VMEM((3, 2, 2, hidden, half), BF16),
             pltpu.VMEM((groups, group_rows, half), BF16),
             pltpu.VMEM((groups, group_rows, half), BF16),
-            pltpu.VMEM((groups, group_rows, half), F32),
+            pltpu.VMEM((2, groups, group_rows, half), F32),
             pltpu.VMEM((groups, group_rows, half), F32),
             pltpu.VMEM((groups, group_rows, 128), F32),
             pltpu.VMEM((2, groups, group_rows, hidden), F32),
             pltpu.VMEM((2, peers, cap, part), BF16),
             pltpu.VMEM((2, peers, cap, part), BF16),
-            pltpu.VMEM((groups, peers // groups, 128), F32),
+            pltpu.VMEM((2, groups, peers // groups, 128), F32),
             pltpu.VMEM((groups, peers // groups, 128), F32),
             pltpu.VMEM((peers, 1, 128), F32),
             pltpu.VMEM((2, peers, 1, 128), F32),
@@ -531,6 +567,10 @@
             dma((2, groups)),
             dma((groups,)),
             dma((groups,)),
+            dma((2, groups)),
+            dma((2, groups)),
+            dma((2, groups)),
+            dma((2, groups)),
             pltpu.SemaphoreType.REGULAR,
         ],
         compiler_params=pltpu.CompilerParams(

time: 125 us -> 120 us (0.960)
  Pallas kernels: 122 us -> 117 us
    pallas_call x1, Pallas kernels: 122 us -> 117 us  [body(): pl.pallas_call(functools.partial(kernel, ny, nz), name='experts', out_sha...]
where the time goes in v5:
time: 120 us
  Pallas kernels  117 us (98%)
  local copies, waits for them, and re-layouts  2.17 us (2%)
    pallas_call x1, Pallas kernels, body(): pl.pallas_call(functools.partial(kernel, ny, nz), name='experts', out_sha...  117 us

profile of v5, /device:TPU:1, one launch (start us, length us, event | category | flops | bytes accessed | tf_op | source)
XLA Modules:
  0.0 119.9 jit_solution(11244675294298695526)
XLA Ops:
  0.6 117.1 %experts.1 = (bf16[128,512]{1,0:T(8,128)(2,1)}, f32[8,128]{1,0:T(8,128)}) custom-call(s32[8,128]{1,0:T(8,128)} %bitcast.10, f32[8,128]{1,0:T(8,128)} %bitcast.11, f32[1,128]{1,0:T(1,128)} %bitcast.13, bf16[128,512]{1,0:T(8,128)(2,1)} %ck.1, bf16[128,512]{1,0:T(8,128)(2,1)} %og.1, bf16[192,2048]{1,0:T(8,128)(2,1)} %bitcast.7, bf16[192,2048]{1,0:T(8,128)(2,1)} %bitcast.8, ...), custom_call_target="tpu_custom_call" | custom-call | tf_op jit(solution)/shard_map/experts/pallas_call | solution.py:524
  117.7 0.0 copy-start
  117.7 1.6 %copy.12 = bf16[128,512]{1,0:T(8,128)(2,1)} copy(bf16[128,512]{1,0:T(8,128)(2,1)} %get-tuple-element.8) | data formatting | bytes 262144
  119.3 0.0 copy-done
  119.3 0.6 copy.13
Async XLA Ops:
  117.7 1.6 %copy-start = (f32[8,128]{1,0:T(8,128)S(1)}, f32[8,128]{1,0:T(8,128)}, u32[]{:S(2)}) copy-start(f32[8,128]{1,0:T(8,128)} %get-tuple-element.5) | copy-start | bytes 12292

commit v6 on v5

--- a/solution.py
+++ b/solution.py
@@ -66,6 +66,8 @@
     term_in,
     term_ret,
     term_came,
+    part_t,
+    part_in,
     loc_sem,
     a_send,
     a_recv,
@@ -87,6 +89,8 @@
     c_recv,
     k_send,
     k_recv,
+    x_send,
+    x_recv,
     ready,
 ):
     order = send_order(ny, nz)
@@ -162,7 +166,8 @@
         pl.semaphore_signal(barrier, inc=1, device_id={"tensor": (x + step) % 4})
     pl.semaphore_signal(barrier, inc=1, device_id=sibling)
     pl.semaphore_signal(barrier, inc=1, device_id={"tensor": 3 - x, "dp": 1 - dp})
-    each(0, peers, lambda n: pl.semaphore_signal(barrier, inc=1, device_id=target(n)))
+    for n in sorted(range(1, peers), key=lambda n: -sum(min(d, m - d) for d, m in zip(order[n], (ny, nz)))):
+        pl.semaphore_signal(barrier, inc=1, device_id=target(n))
 
     r = lax.broadcasted_iota(jnp.int32, (peers, tokens), 0)
     expert = jnp.zeros((peers, tokens), jnp.int32)
@@ -264,6 +269,13 @@
         copy.start()
     dispatch(me, 0)
     choose(1)
+    ahead = min(3, groups - 1)
+
+    def forward_own(g, carry):
+        forward(me, 0, g)
+        return carry
+
+    lax.fori_loop(0, ahead, forward_own, 0)
     for i in range(2):
         remote(ck, raw.at[mate, i], a_send.at[i], a_recv.at[i], a_peer).wait_recv()
     build(mate)
@@ -326,11 +338,7 @@
         term_part[where] = jnp.broadcast_to(term, (n_rows, 128)).reshape(small, per * cap, 128)
         early(first, small, 0)
 
-    def forward_own(g, carry):
-        forward(me, 0, g)
-        return carry
-
-    lax.fori_loop(0, groups, forward_own, 0)
+    lax.fori_loop(ahead, groups, forward_own, 0)
     for i in range(2, 8):
         local[i].wait()
     weight_landed(0)
@@ -364,31 +372,42 @@
             remote(term_half.at[0, g], term_half.at[1, g], k_send.at[1, g], k_recv.at[1, g], sibling),
         )
 
+    def give_terms(g):
+        @pl.when(a == 1)
+        def _():
+            to_sibling(g)[1].wait_recv()
+
+        remote(term_half.at[0, g], term_in.at[g], t_send.at[g], t_recv.at[g], b_peer).wait_recv()
+        term_ret[pl.ds(g * per, per)] = (term_half[a, g] + term_in[g])[:, None, :]
+
+        def send(n):
+            remote(
+                term_ret.at[n], term_came.at[n], s_send.at[g], s_recv.at[g], origin(n, x)
+            ).start()
+
+        each(g * per, per, send)
+
     def give_back(g):
         @pl.when(a == 1)
         def _():
-            for copy in to_sibling(g):
-                copy.wait_recv()
+            to_sibling(g)[0].wait_recv()
 
         remote(psend.at[g], pin.at[g], p_send.at[g], p_recv.at[g], b_peer).wait_recv()
-        remote(term_half.at[0, g], term_in.at[g], t_send.at[g], t_recv.at[g], b_peer).wait_recv()
         total = (keep[a, g] + pin[g].astype(F32)).reshape(per, cap, half).astype(BF16)
         where = pl.ds(g * per, per)
         for q in range(2):
             ret[q, where] = total[:, :, q * part : (q + 1) * part]
-        term_ret[where] = (term_half[a, g] + term_in[g])[:, None, :]
 
         def send(side, n):
             q, plane = ((me, x), (mate, 2 * h + mate))[side]
             to = origin(n, plane)
             remote(ret.at[q, n], came.at[side, n], r_send.at[side, g], r_recv.at[side, g], to).start()
-            remote(
-                term_ret.at[n], term_came.at[side, n], s_send.at[side, g], s_recv.at[side, g], to
-            ).start()
 
         for n in range(g * per, g * per + per):
             send(1, n)
             each(n, 1, functools.partial(send, 0))
+        for early in (range(0, min(2, groups)) if g == 0 else range(g + 1, min(g + 2, groups))):
+            give_terms(early)
 
     def mate_quarter(c, carry):
         first = c * small
@@ -399,11 +418,6 @@
             pre[1, where].reshape(n_rows, -1),
             product(first, small, 1, 2, mate),
         )
-        psend[where] = (other_part[where] + results(d_gate, d_up, mate, 1 - h, small)).astype(BF16)
-        for i in range(small):
-            g = first + i
-            remote(psend.at[g], pin.at[g], p_send.at[g], p_recv.at[g], b_peer).start()
-        keep[0, where] = keep[0, where] + results(d_gate, d_up, mate, h, small)
         term = term_part[where].reshape(n_rows, 128) + term
         lane = lax.broadcasted_iota(jnp.int32, (small * per, cap, 128), 2)
         at = lax.broadcasted_iota(jnp.int32, (small * per, cap, 128), 1)
@@ -415,58 +429,26 @@
 
             @pl.when(a == 1)
             def _():
-                for copy in to_sibling(g):
-                    copy.start()
+                to_sibling(first + i)[1].start()
+
+        psend[where] = (other_part[where] + results(d_gate, d_up, mate, 1 - h, small)).astype(BF16)
+        for i in range(small):
+            g = first + i
+            remote(psend.at[g], pin.at[g], p_send.at[g], p_recv.at[g], b_peer).start()
+        keep[0, where] = keep[0, where] + results(d_gate, d_up, mate, h, small)
+        for i in range(small):
+
+            @pl.when(a == 1)
+            def _():
+                to_sibling(first + i)[0].start()
+
         return carry
 
     lax.fori_loop(0, steps, mate_quarter, 0)
-    pl.semaphore_wait(ready, 1)
-    for g in range(groups):
-        give_back(g)
-
-    came[0, 0] = ret[me, 0]
-    term_came[0, 0] = term_ret[0]
-
-    def returned(g, ref, side, sends, recvs):
-        act = lambda ref: remote(ref, ref, sends.at[side, g], recvs.at[side, g], b_peer).wait_recv()
-        if side == 0:
-            one_wait(g, ref.at[0], act)
-        else:
-            act(ref.at[1, pl.ds(g * per, per)])
-
-    def landed(g, carry):
-        for side in range(2):
-            returned(g, came, side, r_send, r_recv)
-            returned(g, term_came, side, s_send, s_recv)
-        return carry
-
-    lax.fori_loop(0, groups, landed, 0)
-    mixed = 0.0
-    for side in range(2):
-        back_rows = came[side].astype(F32).reshape(peers * cap, part).astype(BF16)
-        mixed += jnp.dot(mix_hi[side], back_rows, preferred_element_type=F32)
-        mixed += jnp.dot(mix_lo[side], back_rows, preferred_element_type=F32)
-    out[...] = mixed.astype(BF16)
-
-    lane = lax.broadcasted_iota(jnp.int32, (peers, cap, 128), 2)
-    at = lax.broadcasted_iota(jnp.int32, (peers, cap, 128), 1)
-    by_expert = []
-    for side in range(2):
-        line = term_came[side].reshape(peers, 128)
-        seen = jnp.sum(jnp.where(lane == at, line[:, None, :], 0.0), axis=2, keepdims=True)
-        chosen = hot[side].astype(F32).reshape(peers, cap, tokens)
-        by_expert.append(jnp.sum(chosen * seen, axis=1))
-    for k in range(picks):
-        total = 0.0
-        for side in range(2):
-            same = ids[pl.ds(k, 1), :] == experts[side]
-            total += jnp.sum(jnp.where(same, by_expert[side], 0.0), axis=0, keepdims=True)
-        terms_out[pl.ds(k, 1), :] = total
-
     for copy in a_copies:
         copy.wait_send()
 
-    def drain(g, carry):
+    def drain_rows(g, carry):
         for turn, q in enumerate((me, mate)):
             one_wait(
                 g,
@@ -480,6 +462,61 @@
             def _():
                 remote(ref, ref, c_send.at[turn, g], c_recv.at[turn, g], sibling).wait_send()
 
+        return carry
+
+    lax.fori_loop(0, groups, drain_rows, 0)
+    pl.semaphore_wait(ready, 1)
+    for g in range(groups):
+        give_back(g)
+
+    came[0, 0] = ret[me, 0]
+    term_came[0] = term_ret[0]
+
+    def returned(g, ref, side, sends, recvs):
+        act = lambda ref: remote(ref, ref, sends.at[side, g], recvs.at[side, g], b_peer).wait_recv()
+        if side == 0:
+            one_wait(g, ref.at[0], act)
+        else:
+            act(ref.at[1, pl.ds(g * per, per)])
+
+    def landed(g, carry):
+        for side in range(2):
+            returned(g, came, side, r_send, r_recv)
+        return carry
+
+    mixed = 0.0
+    cuts = (0, groups - groups // 4, groups) if groups > 4 else (0, groups)
+    for first, last in zip(cuts, cuts[1:]):
+        if last == groups:
+            def terms_landed(g, carry):
+                one_wait(
+                    g, term_came, lambda ref: remote(ref, ref, s_send.at[g], s_recv.at[g], a_peer).wait_recv()
+                )
+                return carry
+
+            lax.fori_loop(0, groups, terms_landed, 0)
+            lane = lax.broadcasted_iota(jnp.int32, (peers, cap, 128), 2)
+            at = lax.broadcasted_iota(jnp.int32, (peers, cap, 128), 1)
+            line = term_came[...].reshape(peers, 128)
+            seen = jnp.sum(jnp.where(lane == at, line[:, None, :], 0.0), axis=2, keepdims=True)
+            by_expert = jnp.sum(hot[0].astype(F32).reshape(peers, cap, tokens) * seen, axis=1)
+            for k in range(picks):
+                same = ids[pl.ds(k, 1), :] == experts[0]
+                part_t[pl.ds(k, 1), :] = jnp.sum(jnp.where(same, by_expert, 0.0), axis=0, keepdims=True)
+            swap = remote(part_t, part_in, x_send.at[0], x_recv.at[0], a_peer)
+            swap.start()
+        lax.fori_loop(first, last, landed, 0)
+        lanes = slice(first * per * cap, last * per * cap)
+        for side in range(2):
+            back_rows = came[side, first * per : last * per].astype(F32)
+            back_rows = back_rows.reshape((last - first) * per * cap, part).astype(BF16)
+            mixed += jnp.dot(mix_hi[side, :, lanes], back_rows, preferred_element_type=F32)
+            mixed += jnp.dot(mix_lo[side, :, lanes], back_rows, preferred_element_type=F32)
+    out[...] = mixed.astype(BF16)
+    swap.wait()
+    terms_out[...] = part_t[...] + part_in[...]
+
+    def drain(g, carry):
         for side, q in enumerate((me, mate)):
             if side == 0:
                 one_wait(
@@ -490,12 +527,11 @@
                 one_wait(
                     g,
                     term_ret,
-                    lambda ref: remote(ref, ref, s_send.at[0, g], s_recv.at[0, g], b_peer).wait_send(),
+                    lambda ref: remote(ref, ref, s_send.at[g], s_recv.at[g], b_peer).wait_send(),
                 )
             else:
-                for ref, sends, recvs in ((ret.at[q], r_send, r_recv), (term_ret, s_send, s_recv)):
-                    ref = ref.at[pl.ds(g * per, per)]
-                    remote(ref, ref, sends.at[1, g], recvs.at[1, g], b_peer).wait_send()
+                ref = ret.at[q, pl.ds(g * per, per)]
+                remote(ref, ref, r_send.at[1, g], r_recv.at[1, g], b_peer).wait_send()
         remote(term_half.at[0, g], term_in.at[g], t_send.at[g], t_recv.at[g], b_peer).wait_send()
 
         @pl.when(a == 1)
@@ -549,7 +585,9 @@
             pltpu.VMEM((2, groups, peers // groups, 128), F32),
             pltpu.VMEM((groups, peers // groups, 128), F32),
             pltpu.VMEM((peers, 1, 128), F32),
-            pltpu.VMEM((2, peers, 1, 128), F32),
+            pltpu.VMEM((peers, 1, 128), F32),
+            pltpu.VMEM((picks, tokens), F32),
+            pltpu.VMEM((picks, tokens), F32),
             dma((8,)),
             dma((2,)),
             dma((2,)),
@@ -563,14 +601,16 @@
             dma((groups,)),
             dma((2, groups)),
             dma((2, groups)),
-            dma((2, groups)),
-            dma((2, groups)),
             dma((groups,)),
             dma((groups,)),
-            dma((2, groups)),
-            dma((2, groups)),
-            dma((2, groups)),
-            dma((2, groups)),
+            dma((groups,)),
+            dma((groups,)),
+            dma((2, groups)),
+            dma((2, groups)),
+            dma((2, groups)),
+            dma((2, groups)),
+            dma((1,)),
+            dma((1,)),
             pltpu.SemaphoreType.REGULAR,
         ],
         compiler_params=pltpu.CompilerParams(

time: 120 us -> 119 us (level)
  no operation moved by 1% of the time
where the time goes in v6:
time: 119 us
  Pallas kernels  116 us (97%)
  local copies, waits for them, and re-layouts  2.17 us (2%)
    pallas_call x1, Pallas kernels, body(): pl.pallas_call(functools.partial(kernel, ny, nz), name='experts', out_sha...  116 us

profile of v6, /device:TPU:1, one launch (start us, length us, event | category | flops | bytes accessed | tf_op | source)
XLA Modules:
  0.0 118.7 jit_solution(5858944883779085170)
XLA Ops:
  0.6 115.9 %experts.1 = (bf16[128,512]{1,0:T(8,128)(2,1)}, f32[8,128]{1,0:T(8,128)}) custom-call(s32[8,128]{1,0:T(8,128)} %bitcast.10, f32[8,128]{1,0:T(8,128)} %bitcast.11, f32[1,128]{1,0:T(1,128)} %bitcast.13, bf16[128,512]{1,0:T(8,128)(2,1)} %ck.1, bf16[128,512]{1,0:T(8,128)(2,1)} %og.1, bf16[192,2048]{1,0:T(8,128)(2,1)} %bitcast.7, bf16[192,2048]{1,0:T(8,128)(2,1)} %bitcast.8, ...), custom_call_target="tpu_custom_call" | custom-call | tf_op jit(solution)/shard_map/experts/pallas_call | solution.py:560
  116.5 0.0 copy-start
  116.6 1.6 %copy.12 = bf16[128,512]{1,0:T(8,128)(2,1)} copy(bf16[128,512]{1,0:T(8,128)(2,1)} %get-tuple-element.8) | data formatting | bytes 262144
  118.1 0.0 copy-done
  118.1 0.6 copy.13
Async XLA Ops:
  116.5 1.6 %copy-start = (f32[8,128]{1,0:T(8,128)S(1)}, f32[8,128]{1,0:T(8,128)}, u32[]{:S(2)}) copy-start(f32[8,128]{1,0:T(8,128)} %get-tuple-element.5) | copy-start | bytes 12292

commit v7 on v6

--- a/solution.py
+++ b/solution.py
@@ -442,8 +442,11 @@
             def _():
                 to_sibling(first + i)[0].start()
 
+        for early in range(min(1, steps - 2)):
+            pl.when(c == early + 2)(functools.partial(give_back, early))
         return carry
 
+    pl.semaphore_wait(ready, 1)
     lax.fori_loop(0, steps, mate_quarter, 0)
     for copy in a_copies:
         copy.wait_send()
@@ -465,8 +468,7 @@
         return carry
 
     lax.fori_loop(0, groups, drain_rows, 0)
-    pl.semaphore_wait(ready, 1)
-    for g in range(groups):
+    for g in range(max(0, min(1, steps - 2)), groups):
         give_back(g)
 
     came[0, 0] = ret[me, 0]

time: 119 us -> 119 us (level)
  no operation moved by 1% of the time
where the time goes in v7:
time: 119 us; the launch traced here: 118 us
  Pallas kernels  116 us (97%)
  local copies, waits for them, and re-layouts  2.17 us (2%)
    pallas_call x1, Pallas kernels, body(): pl.pallas_call(functools.partial(kernel, ny, nz), name='experts', out_sha...  116 us

profile of v7, /device:TPU:1, one launch (start us, length us, event | category | flops | bytes accessed | tf_op | source)
XLA Modules:
  0.0 118.4 jit_solution(16413820761978794500)
XLA Ops:
  0.6 115.6 %experts.1 = (bf16[128,512]{1,0:T(8,128)(2,1)}, f32[8,128]{1,0:T(8,128)}) custom-call(s32[8,128]{1,0:T(8,128)} %bitcast.10, f32[8,128]{1,0:T(8,128)} %bitcast.11, f32[1,128]{1,0:T(1,128)} %bitcast.13, bf16[128,512]{1,0:T(8,128)(2,1)} %ck.1, bf16[128,512]{1,0:T(8,128)(2,1)} %og.1, bf16[192,2048]{1,0:T(8,128)(2,1)} %bitcast.7, bf16[192,2048]{1,0:T(8,128)(2,1)} %bitcast.8, ...), custom_call_target="tpu_custom_call" | custom-call | tf_op jit(solution)/shard_map/experts/pallas_call | solution.py:562
  116.2 0.0 copy-start
  116.3 1.6 %copy.12 = bf16[128,512]{1,0:T(8,128)(2,1)} copy(bf16[128,512]{1,0:T(8,128)(2,1)} %get-tuple-element.8) | data formatting | bytes 262144
  117.8 0.0 copy-done
  117.8 0.6 copy.13
Async XLA Ops:
  116.2 1.6 %copy-start = (f32[8,128]{1,0:T(8,128)S(1)}, f32[8,128]{1,0:T(8,128)}, u32[]{:S(2)}) copy-start(f32[8,128]{1,0:T(8,128)} %get-tuple-element.5) | copy-start | bytes 12292
